TPU v7x, 512 devices: a whole 4x4x16 slice. The times are simulated.
512 devices in a mesh: rng: 16 (over y, z_hi), azi: 32 (over x, z_lo, core).
Axes of the slice: x: 4, y: 4, z: 16 (z_hi: 4, z_lo: 4; z = z_hi * 4 + z_lo), core: 2. Of those that a mesh axis runs over, the one named last changes fastest.
Arguments:
- observed: float32 [2048, 8192], P('rng', 'azi'), may hold values from -6 to 6
- psf_tiles: float32 [16, 64, 121], P('rng', 'azi'), may hold values from 0.002 to 0.02
Outputs:
- estimate: float32 [2048, 8192], P('rng', 'azi')
- residual: float32 [2048, 8192], P('rng', 'azi')
All inputs are finite; a program needn't handle non-finite values.
Results may differ from a plain program's by a relative error of at most 0.00035.
Values sent between devices are 32-bit elements; how exact they have to be, the bound alone decides.
A program may use at most 64 MiB of HBM per device.

v0:
```python
import jax
import jax.numpy as jnp
from jax import lax
from jax.sharding import PartitionSpec as P

TILE = 128
KSIZE = 11
ITERS = 2


def passed_along(block, axis, distance):
    devices = range(lax.axis_size(axis))
    route = [(i - distance, i) for i in devices if i - distance in devices]
    return lax.ppermute(block, axis, route)


def padded(block, sides, width):
    for axis, dim in sides:
        count = lax.axis_size(axis)
        forward = [(i, i + 1) for i in range(count - 1)]
        backward = [(target, source) for source, target in forward]
        low = lax.ppermute(
            lax.slice_in_dim(block, block.shape[dim] - width, None, axis=dim), axis, forward
        )
        high = lax.ppermute(lax.slice_in_dim(block, 0, width, axis=dim), axis, backward)
        block = jnp.concatenate([low, block, high], axis=dim)
    return block


def band_matrices(psf_tiles):
    tiles_r, tiles_c = (psf_tiles.shape[0], psf_tiles.shape[1])
    kernels = psf_tiles.reshape(tiles_r, tiles_c, KSIZE, KSIZE)
    span_cols = TILE + KSIZE - 1
    col_idx = lax.broadcasted_iota(jnp.int32, (KSIZE, span_cols, TILE), 1)
    out_idx = lax.broadcasted_iota(jnp.int32, (KSIZE, span_cols, TILE), 2)
    tap_idx = lax.broadcasted_iota(jnp.int32, (KSIZE, span_cols, TILE), 0)
    selector = (col_idx - out_idx == tap_idx).astype(jnp.float32)
    return jnp.einsum("abuv,vcj->uabcj", kernels, selector, precision=lax.Precision.HIGHEST)


def blur_local(field_ext, band_mats):
    radius = (KSIZE - 1) // 2
    tiles_r, tiles_c = (band_mats.shape[1], band_mats.shape[2])
    span_cols = band_mats.shape[3]
    row_count = field_ext.shape[0] - 2 * radius
    windows = jnp.stack(
        [
            field_ext[:, column_tile * TILE : column_tile * TILE + span_cols]
            for column_tile in range(tiles_c)
        ]
    )
    summed = jnp.zeros((tiles_r, TILE, tiles_c, TILE), jnp.float32)
    for offset in range(KSIZE):
        window_rows = windows[:, offset : offset + row_count, :].reshape(
            tiles_c, tiles_r, TILE, span_cols
        )
        summed = summed + jnp.einsum(
            "barc,abcj->arbj", window_rows, band_mats[offset], precision=lax.Precision.HIGHEST
        )
    return summed.reshape(row_count, tiles_c * TILE)


def adjoint_local(field, band_mats):
    radius = (KSIZE - 1) // 2
    tiles_r, tiles_c = (band_mats.shape[1], band_mats.shape[2])
    span_cols = band_mats.shape[3]
    row_count, col_count = field.shape
    shaped = field.reshape(tiles_r, TILE, tiles_c, TILE)
    extended = jnp.zeros((row_count + 2 * radius, col_count + 2 * radius), jnp.float32)
    for offset in range(KSIZE):
        spread = jnp.einsum(
            "arbj,abcj->arbc", shaped, band_mats[offset], precision=lax.Precision.HIGHEST
        )
        for column_tile in range(tiles_c):
            piece = spread[:, :, column_tile, :].reshape(row_count, span_cols)
            extended = extended.at[
                offset : offset + row_count, column_tile * TILE : column_tile * TILE + span_cols
            ].add(piece)
    return extended


def fold_rims(extended):
    radius = (KSIZE - 1) // 2
    top_strip = extended[:radius]
    low_strip = extended[-radius:]
    from_below = passed_along(top_strip, "rng", -1)
    from_above = passed_along(low_strip, "rng", 1)
    inner = extended[radius:-radius]
    inner = inner.at[-radius:].add(from_below).at[:radius].add(from_above)
    left_strip = inner[:, :radius]
    right_strip = inner[:, -radius:]
    from_right = passed_along(left_strip, "azi", -1)
    from_left = passed_along(right_strip, "azi", 1)
    inner = (
        inner.at[:, -2 * radius : -radius].add(from_right).at[:, radius : 2 * radius].add(from_left)
    )
    return inner[:, radius:-radius]


def with_rims(field):
    radius = (KSIZE - 1) // 2
    return padded(field, (("rng", 0), ("azi", 1)), radius)


def gradient_pair(residual, band_mats):
    block = fold_rims(adjoint_local(residual, band_mats))
    return (block, block)


def rimmed(block):
    return with_rims(block)


def grad_norm(gradient):
    return lax.psum(jnp.sum(gradient * gradient), ("rng", "azi"))


def body(observed, psf_tiles):
    band_mats = band_matrices(psf_tiles)
    estimate = jnp.zeros_like(observed)
    residual = observed
    direction = jnp.zeros_like(observed)
    image = jnp.zeros_like(observed)
    gamma = jnp.float32(1.0)
    delta = jnp.float32(0.0)
    for step in range(ITERS):
        gradient, gradient_wide = gradient_pair(residual, band_mats)
        gamma_new = grad_norm(gradient)
        factor = gamma_new / gamma
        direction = gradient + factor * direction
        gamma = gamma_new
        image = blur_local(rimmed(direction), band_mats)
        delta = lax.psum(jnp.sum(image * image), ("rng", "azi"))
        alpha = gamma / delta
        estimate = estimate + alpha * direction
        residual = residual - alpha * image
    return (estimate, residual)


def solution(mesh):
    return jax.shard_map(
        body,
        mesh=mesh,
        in_specs=(P("rng", "azi"), P("rng", "azi", None)),
        out_specs=(P("rng", "azi"), P("rng", "azi")),
        check_vma=False,
    )
```

profile of v0, /device:TPU:1, one launch (start us, length us, event | category | flops | bytes accessed | tf_op | source)
XLA Modules:
  0.0 684.0 jit_solution(6028751747108717199)
XLA Ops:
  7.6 3.0 scatter-add.175
  10.8 2.1 scatter-add.176
  55.5 10.3 %collective-permute-start.1 = (f32[5,266]{0,1:T(8,128)S(1)}, f32[5,266]{0,1:T(8,128)S(1)}, u32[]{:S(2)}, u32[]{:S(2)}) collective-permute-start(f32[5,266]{0,1:T(8,128)S(1)} %get-tuple-element.651), channel_id=1, source_target_pairs={{0,32},{32,64},{64,96},{96,128},{128,160},{160,192},{192,224},{224... | collective-permute-start | bytes 15968 | tf_op jit(solution)/shard_map/ppermute | solution.py:14
  65.8 5.8 collective-permute-done
  73.4 7.6 %collective-permute-start.2 = (f32[128,5]{0,1:T(8,128)S(1)}, f32[128,5]{0,1:T(8,128)S(1)}, u32[]{:S(2)}, u32[]{:S(2)}) collective-permute-start(f32[128,5]{0,1:T(8,128)S(1)} %get-tuple-element.656), channel_id=1, source_target_pairs={{1,0},{2,1},{3,2},{4,3},{5,4},{6,5},{7,6},{8,7},{9,8},{10,9},{11,1... | collective-permute-start | bytes 7688 | tf_op jit(solution)/shard_map/ppermute | solution.py:14
  86.9 116.0 %psum.28 = f32[]{:T(128)} all-reduce(f32[]{:T(128)} %multiply_reduce_fusion.3), channel_id=1, replica_groups=mesh['rng'=16,'azi'=32] {'rng','azi'}, use_global_device_ids=true, to_apply=%region_4.0 | all-reduce | flops 1 | bytes 8 | tf_op jit(solution)/shard_map/psum | solution.py:115
  203.7 3.8 collective-permute-start.4
  209.8 17.0 %collective-permute-done.5 = f32[5,256]{0,1:T(8,128)S(1)} collective-permute-done((f32[5,256]{0,1:T(8,128)S(1)}, f32[5,256]{0,1:T(8,128)S(1)}, u32[]{:S(2)}, u32[]{:S(2)}) %collective-permute-start.5) | collective-permute-done | bytes 5152 | tf_op jit(solution)/shard_map/ppermute | solution.py:25
  228.8 2.4 collective-permute-start.7
  231.2 2.6 collective-permute-done.7
  242.4 106.2 %psum.29 = f32[]{:T(128)} all-reduce(f32[]{:T(128)} %get-tuple-element.663), channel_id=1, replica_groups=mesh['rng'=16,'azi'=32] {'rng','azi'}, use_global_device_ids=true, to_apply=%region_6.0 | all-reduce | flops 1 | bytes 8 | tf_op jit(solution)/shard_map/psum | solution.py:133
  357.0 2.5 scatter-add.219
  389.1 2.4 scatter-add.244
  402.7 7.9 %collective-permute-start.9 = (f32[5,266]{0,1:T(8,128)S(1)}, f32[5,266]{0,1:T(8,128)S(1)}, u32[]{:S(2)}, u32[]{:S(2)}) collective-permute-start(f32[5,266]{0,1:T(8,128)S(1)} %get-tuple-element.649), channel_id=1, source_target_pairs={{0,32},{32,64},{64,96},{96,128},{128,160},{160,192},{192,224},{224... | collective-permute-start | bytes 15968 | tf_op jit(solution)/shard_map/ppermute | solution.py:14
  410.6 10.2 %collective-permute-done.8 = f32[5,266]{0,1:T(8,128)S(1)} collective-permute-done((f32[5,266]{0,1:T(8,128)S(1)}, f32[5,266]{0,1:T(8,128)S(1)}, u32[]{:S(2)}, u32[]{:S(2)}) %collective-permute-start.8) | collective-permute-done | bytes 5352 | tf_op jit(solution)/shard_map/ppermute | solution.py:14
  422.6 3.1 collective-permute-start.10
  425.7 2.5 collective-permute-start.11
  430.5 104.6 %psum.30 = f32[]{:T(128)} all-reduce(f32[]{:T(128)} %multiply_reduce_fusion.2), channel_id=1, replica_groups=mesh['rng'=16,'azi'=32] {'rng','azi'}, use_global_device_ids=true, to_apply=%region_8.0 | all-reduce | flops 1 | bytes 8 | tf_op jit(solution)/shard_map/psum | solution.py:115
  536.5 5.8 collective-permute-start.12
  543.5 3.6 collective-permute-done.12
  547.1 14.3 %collective-permute-done.13 = f32[5,256]{0,1:T(8,128)S(1)} collective-permute-done((f32[5,256]{0,1:T(8,128)S(1)}, f32[5,256]{0,1:T(8,128)S(1)}, u32[]{:S(2)}, u32[]{:S(2)}) %collective-permute-start.13) | collective-permute-done | bytes 5152 | tf_op jit(solution)/shard_map/ppermute | solution.py:25
  563.4 2.7 collective-permute-start.15
  566.2 2.3 collective-permute-done.15
  576.9 103.6 %psum.31 = f32[]{:T(128)} all-reduce(f32[]{:T(128)} %get-tuple-element.665), channel_id=1, replica_groups=mesh['rng'=16,'azi'=32] {'rng','azi'}, use_global_device_ids=true, to_apply=%region_10.0 | all-reduce | flops 1 | bytes 8 | tf_op jit(solution)/shard_map/psum | solution.py:133
  (196 shorter events, 134.9 us)
Async XLA Ops:
  2.4 1.1 copy-start
  2.4 2.1 copy-start.1
  54.2 17.5 %collective-permute-start = (f32[5,266]{0,1:T(8,128)S(1)}, f32[5,266]{0,1:T(8,128)S(1)}, u32[]{:S(2)}, u32[]{:S(2)}) collective-permute-start(f32[5,266]{0,1:T(8,128)S(1)} %get-tuple-element.652), channel_id=1, source_target_pairs={{32,0},{64,32},{96,64},{128,96},{160,128},{192,160},{224,192},{256... | collective-permute-start | bytes 15968 | tf_op jit(solution)/shard_map/ppermute | solution.py:14
  55.5 17.2 %collective-permute-start.1 = (f32[5,266]{0,1:T(8,128)S(1)}, f32[5,266]{0,1:T(8,128)S(1)}, u32[]{:S(2)}, u32[]{:S(2)}) collective-permute-start(f32[5,266]{0,1:T(8,128)S(1)} %get-tuple-element.651), channel_id=1, source_target_pairs={{0,32},{32,64},{64,96},{96,128},{128,160},{160,192},{192,224},{224... | collective-permute-start | bytes 15968 | tf_op jit(solution)/shard_map/ppermute | solution.py:14
  73.4 10.9 %collective-permute-start.2 = (f32[128,5]{0,1:T(8,128)S(1)}, f32[128,5]{0,1:T(8,128)S(1)}, u32[]{:S(2)}, u32[]{:S(2)}) collective-permute-start(f32[128,5]{0,1:T(8,128)S(1)} %get-tuple-element.656), channel_id=1, source_target_pairs={{1,0},{2,1},{3,2},{4,3},{5,4},{6,5},{7,6},{8,7},{9,8},{10,9},{11,1... | collective-permute-start | bytes 7688 | tf_op jit(solution)/shard_map/ppermute | solution.py:14
  82.4 3.0 collective-permute-start.3
  203.7 6.1 collective-permute-start.4
  207.5 19.3 %collective-permute-start.5 = (f32[5,256]{0,1:T(8,128)S(1)}, f32[5,256]{0,1:T(8,128)S(1)}, u32[]{:S(2)}, u32[]{:S(2)}) collective-permute-start(f32[5,256]{0,1:T(8,128)S(1)} %get-tuple-element.660), channel_id=1, source_target_pairs={{32,0},{64,32},{96,64},{128,96},{160,128},{192,160},{224,192},{256... | collective-permute-start | bytes 15368 | tf_op jit(solution)/shard_map/ppermute | solution.py:25
  226.9 4.3 collective-permute-start.6
  228.8 5.0 collective-permute-start.7
  401.3 19.5 %collective-permute-start.8 = (f32[5,266]{0,1:T(8,128)S(1)}, f32[5,266]{0,1:T(8,128)S(1)}, u32[]{:S(2)}, u32[]{:S(2)}) collective-permute-start(f32[5,266]{0,1:T(8,128)S(1)} %get-tuple-element.650), channel_id=1, source_target_pairs={{32,0},{64,32},{96,64},{128,96},{160,128},{192,160},{224,192},{256... | collective-permute-start | bytes 15968 | tf_op jit(solution)/shard_map/ppermute | solution.py:14
  402.7 19.3 %collective-permute-start.9 = (f32[5,266]{0,1:T(8,128)S(1)}, f32[5,266]{0,1:T(8,128)S(1)}, u32[]{:S(2)}, u32[]{:S(2)}) collective-permute-start(f32[5,266]{0,1:T(8,128)S(1)} %get-tuple-element.649), channel_id=1, source_target_pairs={{0,32},{32,64},{64,96},{96,128},{128,160},{160,192},{192,224},{224... | collective-permute-start | bytes 15968 | tf_op jit(solution)/shard_map/ppermute | solution.py:14
  422.6 5.6 collective-permute-start.10
  425.7 3.3 collective-permute-start.11
  536.5 10.7 %collective-permute-start.12 = (f32[5,256]{0,1:T(8,128)S(1)}, f32[5,256]{0,1:T(8,128)S(1)}, u32[]{:S(2)}, u32[]{:S(2)}) collective-permute-start(f32[5,256]{0,1:T(8,128)S(1)} %get-tuple-element.657), channel_id=1, source_target_pairs={{0,32},{32,64},{64,96},{96,128},{128,160},{160,192},{192,224},{224... | collective-permute-start | bytes 15368 | tf_op jit(solution)/shard_map/ppermute | solution.py:22
  542.2 19.2 %collective-permute-start.13 = (f32[5,256]{0,1:T(8,128)S(1)}, f32[5,256]{0,1:T(8,128)S(1)}, u32[]{:S(2)}, u32[]{:S(2)}) collective-permute-start(f32[5,256]{0,1:T(8,128)S(1)} %get-tuple-element.658), channel_id=1, source_target_pairs={{32,0},{64,32},{96,64},{128,96},{160,128},{192,160},{224,192},{256... | collective-permute-start | bytes 15368 | tf_op jit(solution)/shard_map/ppermute | solution.py:25
  561.5 4.6 collective-permute-start.14
  563.4 5.0 collective-permute-start.15
where the time goes:
time: 688 us; the launch traced here: 684 us
  blocking collectives  430 us (62%)
  local copies, waits for them, and re-layouts  88.9 us (13%)
  waiting for transfers between devices  57.3 us (8%)
  starting transfers between devices  56.9 us (8%)
  matrix products  27.1 us (4%)
  other arithmetic  16.6 us (2%)
    psum x2, blocking collectives, grad_norm(): return lax.psum(jnp.sum(gradient * gradient), ('rng', 'azi'))  221 us
    psum x2, blocking collectives, body(): delta = lax.psum(jnp.sum(image * image), ('rng', 'azi'))  210 us
    scatter-add x44, local copies, waits for them, and re-layouts, adjoint_local(): extended = extended.at[offset:offset + row_count, column_tile * TILE:colu...  81.3 us
    ppermute x4, waiting for transfers between devices, padded(): lax.ppermute(lax.slice_in_dim(block, 0, width, axis=dim), axis, backward)  36.2 us
    ppermute x8, starting transfers between devices, passed_along(): return lax.ppermute(block, axis, route)  35.8 us
    dot_general x22, matrix products, blur_local(): jnp.einsum('barc,abcj->arbj', window_rows, band_mats[offset], precision=l...  16.7 us
    ppermute x8, waiting for transfers between devices, passed_along(): return lax.ppermute(block, axis, route)  16.5 us
  transfers between devices with their start and end apart: 16, of which 10 were waited for; matrix products, arithmetic and copies ran while one was open for 1% of the time, Pallas kernels for 0%

commit v1 on v0

v1 whole, which is shorter than its diff:
```python
import itertools

import jax
import jax.numpy as jnp
from jax import lax
from jax.experimental import pallas as pl
from jax.experimental.pallas import tpu as pltpu
from jax.sharding import PartitionSpec as P

TILE = 128
KSIZE = 11
RADIUS = 5
RIM = 2 * RADIUS
ROWS = 128
COLS = 256
EXT_ROWS = 144
EXT_COLS = 384
PAD = 16
WIDE = KSIZE * TILE
MESH = pl.DeviceIdType.MESH
F32 = jnp.float32
BF16 = jnp.bfloat16

PARTS = {"y": 4, "zh": 4, "x": 4, "zl": 4, "c": 2}
PHASES = (("x", "y", "c"), ("zh", "zl"))
NEIGHBOURS = tuple(
    (dr, da) for dr in (-1, 0, 1) for da in (-1, 0, 1) if (dr, da) != (0, 0)
)


def group_offsets(axes):
    ranges = [range(PARTS[axis]) for axis in axes]
    return [dict(zip(axes, o)) for o in itertools.product(*ranges) if any(o)]


OFFSETS = tuple(group_offsets(axes) for axes in PHASES)


def halves(x):
    high = x.astype(BF16)
    low = (x - high.astype(F32)).astype(BF16)
    return high, low


def kernel(
    obs_ref,
    psf_ref,
    est_ref,
    res_ref,
    taps,
    spread_w,
    gather_w,
    wide,
    tall,
    spill,
    field,
    image,
    grad,
    sides,
    got_rows,
    got_sides,
    got_corners,
    moments,
    got_a,
    got_b,
    halo_send,
    halo_recv,
    sum_send,
    sum_recv,
):
    rng = lax.axis_index("rng")
    azi = lax.axis_index("azi")
    place = {
        "y": rng // 4,
        "zh": rng % 4,
        "x": azi // 8,
        "zl": (azi // 2) % 4,
        "c": azi % 2,
    }

    def member(offset):
        at = {
            axis: lax.rem(place[axis] + offset[axis], PARTS[axis])
            if axis in offset
            else place[axis]
            for axis in PARTS
        }
        return (at["y"] * 4 + at["zh"], at["x"] * 8 + at["zl"] * 2 + at["c"])

    def neighbour(dr, da):
        return (lax.rem(rng + dr + 16, 16), lax.rem(azi + da + 32, 32))

    barrier = pltpu.get_barrier_semaphore()
    partners = [neighbour(*d) for d in NEIGHBOURS]
    partners += [member(o) for offsets in OFFSETS for o in offsets]
    for partner in partners:
        pl.semaphore_signal(barrier, inc=1, device_id=partner, device_id_type=MESH)

    lane = lax.broadcasted_iota(jnp.int32, (TILE, TILE), 1)
    row = lax.broadcasted_iota(jnp.int32, (TILE, TILE), 0)

    taps[...] = jnp.zeros_like(taps)
    taps[0:2, 0 : KSIZE * KSIZE] = psf_ref[0]
    for t in range(2):
        gather_w[t, 3 * TILE :, :] = jnp.zeros((TILE, WIDE), BF16)

        def build(u, packed, t=t):
            line = jnp.broadcast_to(taps[t : t + 1, :], (TILE, TILE))
            line = pltpu.roll(line, lax.rem(2 * TILE - KSIZE * u, TILE), 1)
            line = jnp.where(lane < KSIZE, line, 0.0)
            band = pltpu.roll(line, 0, 1, stride=1, stride_axis=0)
            block = pl.ds(pl.multiple_of(u * TILE, TILE), TILE)
            high, low = halves(jnp.where(lane >= row, band, 0.0))
            spread_w[t, 0:TILE, block] = high
            spread_w[t, TILE : 2 * TILE, block] = high
            spread_w[t, 2 * TILE :, block] = low
            turned = band.T
            high, low = halves(jnp.where(row >= lane, turned, 0.0))
            gather_w[t, 0:TILE, block] = high
            gather_w[t, TILE : 2 * TILE, block] = high
            gather_w[t, 2 * TILE : 3 * TILE, block] = low
            edge = jnp.where(row < lane, turned, 0.0)[0:PAD]
            high, low = halves(edge)
            gather_w[t, 3 * TILE : 3 * TILE + PAD, block] = high
            gather_w[t, 3 * TILE + PAD : 3 * TILE + 2 * PAD, block] = high
            gather_w[t, 3 * TILE + 2 * PAD : 3 * TILE + 3 * PAD, block] = low
            over = jnp.where(lane < row, band, 0.0)
            return packed + pltpu.roll(over, RIM * u, 1)

        packed = lax.fori_loop(0, KSIZE, build, jnp.zeros((TILE, TILE), F32))
        high, low = halves(packed)
        spread_w[t, 0:TILE, WIDE:] = high
        spread_w[t, TILE : 2 * TILE, WIDE:] = high
        spread_w[t, 2 * TILE :, WIDE:] = low
        wide[t, 0:PAD, :] = jnp.zeros((PAD, WIDE + TILE), F32)
        wide[t, PAD + ROWS :, :] = jnp.zeros((PAD, WIDE + TILE), F32)

    def spread(source, out):
        tall_lane = lax.broadcasted_iota(jnp.int32, (EXT_ROWS, TILE), 1)
        over = None
        for t in range(2):
            high, low = halves(source[:, t * TILE : (t + 1) * TILE])
            left = jnp.concatenate([high, low, high], axis=1)
            for n in range(0, WIDE + TILE, 256):
                wide[t, PAD : PAD + ROWS, n : n + 256] = jnp.dot(
                    left, spread_w[t, :, n : n + 256], preferred_element_type=F32
                )
            total = over
            spare = None
            for u in range(KSIZE):
                rows = pl.ds(PAD - u, EXT_ROWS)
                piece = wide[t, rows, u * TILE : (u + 1) * TILE]
                total = piece if total is None else total + piece
                piece = wide[t, rows, WIDE:]
                if u:
                    piece = pltpu.roll(piece, TILE - RIM * u, 1)
                spare = piece if spare is None else spare + piece
            out[:, t * TILE : (t + 1) * TILE] = total
            over = jnp.where(tall_lane < RIM, spare, 0.0)
        out[:, 2 * TILE :] = over

    def gather(source, t):
        tall_lane = lax.broadcasted_iota(jnp.int32, (EXT_ROWS, TILE), 1)
        high, low = halves(source[:, t * TILE : (t + 1) * TILE])
        edge = jnp.where(tall_lane < RIM, source[:, (t + 1) * TILE : (t + 2) * TILE], 0.0)
        edge_high = edge.astype(BF16).astype(F32)
        edge_low = edge - edge_high
        edge = edge_high + pltpu.roll(edge_low, PAD, 1) + pltpu.roll(edge_high, 2 * PAD, 1)
        left = jnp.concatenate([high, low, high, edge.astype(BF16)], axis=1)
        total = None
        for n in range(0, WIDE, 256):
            width = min(256, WIDE - n)
            tall[t, :, n : n + width] = jnp.dot(
                left, gather_w[t, :, n : n + width], preferred_element_type=F32
            )
        for u in range(KSIZE):
            piece = tall[t, pl.ds(u, ROWS), u * TILE : (u + 1) * TILE]
            total = piece if total is None else total + piece
        return total

    def pack(strip):
        out = None
        for k in range(8):
            part = jnp.concatenate(
                [
                    strip[8 * (k + 8 * j) : 8 * (k + 8 * j) + 8]
                    if 8 * (k + 8 * j) < EXT_ROWS
                    else jnp.zeros((8, TILE), F32)
                    for j in range(3)
                ],
                axis=0,
            )
            part = jnp.where(lane[0:24] < PAD, part, 0.0)
            part = pltpu.roll(part, PAD * k, 1) if k else part
            out = part if out is None else out + part
        return out

    def unpack(packed):
        parts = []
        for k in range(8):
            part = pltpu.roll(packed, TILE - PAD * k, 1) if k else packed
            parts.append(jnp.where(lane[0:24] < RIM, part, 0.0))
        return jnp.concatenate(
            [parts[g % 8][8 * (g // 8) : 8 * (g // 8) + 8] for g in range(EXT_ROWS // 8)],
            axis=0,
        )

    def start_exchange(turn):
        out = spill.at[turn]
        sides[turn, 0] = pack(spill[turn, :, 0:TILE])
        sides[turn, 1] = pack(spill[turn, :, 2 * TILE :])
        low, high = pl.ds(0, PAD), pl.ds(ROWS, PAD)
        first, last = pl.ds(0, TILE), pl.ds(2 * TILE, TILE)
        plan = {
            (-1, 0): (out.at[low, :], got_rows.at[turn, 0]),
            (1, 0): (out.at[high, :], got_rows.at[turn, 1]),
            (0, -1): (sides.at[turn, 0], got_sides.at[turn, 0]),
            (0, 1): (sides.at[turn, 1], got_sides.at[turn, 1]),
            (-1, -1): (out.at[low, first], got_corners.at[turn, 0]),
            (-1, 1): (out.at[low, last], got_corners.at[turn, 1]),
            (1, -1): (out.at[high, first], got_corners.at[turn, 2]),
            (1, 1): (out.at[high, last], got_corners.at[turn, 3]),
        }
        copies = []
        for i, d in enumerate(NEIGHBOURS):
            source, target = plan[d]
            copy = pltpu.make_async_remote_copy(
                src_ref=source,
                dst_ref=target,
                send_sem=halo_send.at[turn, i],
                recv_sem=halo_recv.at[turn, i],
                device_id=neighbour(*d),
                device_id_type=MESH,
            )
            copy.start()
            copies.append(copy)
        return copies

    above = jnp.where(rng > 0, 1.0, 0.0)
    below = jnp.where(rng < 15, 1.0, 0.0)
    left_of = jnp.where(azi > 0, 1.0, 0.0)
    right_of = jnp.where(azi < 31, 1.0, 0.0)

    def finish_exchange(turn, copies):
        for copy in copies:
            copy.wait()
        ext = field.at[turn]
        ext[...] = spill[turn]
        strip_row = lax.broadcasted_iota(jnp.int32, (PAD, EXT_COLS), 0)
        strip_lane = lax.broadcasted_iota(jnp.int32, (PAD, TILE), 1)
        corner_row = strip_row[:, 0:TILE]
        ext[:, 0:TILE] += unpack(got_sides[turn, 1]) * left_of
        ext[:, 2 * TILE :] += unpack(got_sides[turn, 0]) * right_of
        ext[0:PAD, :] += jnp.where(strip_row < RIM, got_rows[turn, 1], 0.0) * above
        ext[ROWS:, :] += jnp.where(strip_row < RIM, got_rows[turn, 0], 0.0) * below
        corner = (corner_row < RIM) & (strip_lane < RIM)
        ext[0:PAD, 0:TILE] += jnp.where(corner, got_corners[turn, 3], 0.0) * (above * left_of)
        ext[0:PAD, 2 * TILE :] += jnp.where(corner, got_corners[turn, 2], 0.0) * (above * right_of)
        ext[ROWS:, 0:TILE] += jnp.where(corner, got_corners[turn, 1], 0.0) * (below * left_of)
        ext[ROWS:, 2 * TILE :] += jnp.where(corner, got_corners[turn, 0], 0.0) * (below * right_of)
        r = lax.broadcasted_iota(jnp.int32, (EXT_ROWS, EXT_COLS), 0)
        c = lax.broadcasted_iota(jnp.int32, (EXT_ROWS, EXT_COLS), 1)
        inside = (
            (r >= jnp.where(rng == 0, RADIUS, 0))
            & (r < jnp.where(rng == 15, ROWS + RADIUS, EXT_ROWS))
            & (c >= jnp.where(azi == 0, RADIUS, 0))
            & (c < jnp.where(azi == 31, COLS + RADIUS, EXT_COLS))
        )
        ext[...] = jnp.where(inside, ext[...], 0.0)

    def square_sum(x):
        return jnp.sum(jnp.sum(x * x, axis=0, keepdims=True), axis=1, keepdims=True)

    def own_squares(turn):
        r = lax.broadcasted_iota(jnp.int32, (EXT_ROWS, EXT_COLS), 0)
        c = lax.broadcasted_iota(jnp.int32, (EXT_ROWS, EXT_COLS), 1)
        own = (r >= RADIUS) & (r < ROWS + RADIUS) & (c >= RADIUS) & (c < COLS + RADIUS)
        return square_sum(jnp.where(own, field[turn], 0.0))

    def own_block(turn):
        grad[turn] = pltpu.roll(field[turn], EXT_COLS - RADIUS, 1)[:, 0:COLS]

    spread(obs_ref[...], spill.at[0])
    pl.semaphore_wait(barrier, len(partners))
    first = start_exchange(0)
    finish_exchange(0, first)
    for t in range(2):
        image[0, :, t * TILE : (t + 1) * TILE] = gather(field.at[0], t)
    spread(image[0], spill.at[1])
    second = start_exchange(1)
    gamma = own_squares(0)
    delta = square_sum(image[0])
    own_block(0)
    finish_exchange(1, second)
    for t in range(2):
        image[1, :, t * TILE : (t + 1) * TILE] = gather(field.at[1], t)
    omega = own_squares(1)
    pi = square_sum(image[1])
    line = lane[0:1]
    moments[0] = jnp.where(
        line == 0, gamma, jnp.where(line == 1, delta, jnp.where(line == 2, omega, pi))
    )
    for phase, got in enumerate((got_a, got_b)):
        for i, o in enumerate(OFFSETS[phase]):
            pltpu.make_async_remote_copy(
                src_ref=moments.at[phase],
                dst_ref=got.at[i],
                send_sem=sum_send.at[phase],
                recv_sem=sum_recv.at[phase],
                device_id=member(o),
                device_id_type=MESH,
            ).start()
        if phase == 0:
            own_block(1)
        pltpu.make_async_copy(got, got, sum_recv.at[phase]).wait()
        moments[phase + 1] = moments[phase] + jnp.sum(got[...], axis=0)
    total = moments[2]
    gamma, delta, omega, pi = (total[:, i : i + 1] for i in range(4))
    alpha = gamma / delta
    rise = alpha * (omega / delta)
    alpha_1 = (omega - delta * (delta / gamma)) / (pi - omega * (omega / delta))
    near = alpha + alpha_1 * rise
    far = alpha * alpha_1
    own = pl.ds(RADIUS, ROWS)
    est_ref[...] = near * grad[0, own, :] - far * grad[1, own, :]
    res_ref[...] = obs_ref[...] - near * image[0] + far * image[1]
    for phase, got in enumerate((got_a, got_b)):
        pltpu.make_async_copy(got, got, sum_send.at[phase]).wait()


def body(observed, psf_tiles):
    block = jax.ShapeDtypeStruct((ROWS, COLS), F32)
    vmem = pl.BlockSpec(memory_space=pltpu.VMEM)
    return pl.pallas_call(
        kernel,
        out_shape=(block, block),
        in_specs=[vmem, vmem],
        out_specs=(vmem, vmem),
        scratch_shapes=[
            pltpu.VMEM((8, TILE), F32),
            pltpu.VMEM((2, 3 * TILE, WIDE + TILE), BF16),
            pltpu.VMEM((2, 4 * TILE, WIDE), BF16),
            pltpu.VMEM((2, ROWS + 2 * PAD, WIDE + TILE), F32),
            pltpu.VMEM((2, EXT_ROWS, WIDE), F32),
            pltpu.VMEM((2, EXT_ROWS, EXT_COLS), F32),
            pltpu.VMEM((2, EXT_ROWS, EXT_COLS), F32),
            pltpu.VMEM((2, ROWS, COLS), F32),
            pltpu.VMEM((2, EXT_ROWS, COLS), F32),
            pltpu.VMEM((2, 2, 24, TILE), F32),
            pltpu.VMEM((2, 2, PAD, EXT_COLS), F32),
            pltpu.VMEM((2, 2, 24, TILE), F32),
            pltpu.VMEM((2, 4, PAD, TILE), F32),
            pltpu.VMEM((3, 1, TILE), F32),
            pltpu.VMEM((len(OFFSETS[0]), 1, TILE), F32),
            pltpu.VMEM((len(OFFSETS[1]), 1, TILE), F32),
            pltpu.SemaphoreType.DMA((2, 8)),
            pltpu.SemaphoreType.DMA((2, 8)),
            pltpu.SemaphoreType.DMA((2,)),
            pltpu.SemaphoreType.DMA((2,)),
        ],
        compiler_params=pltpu.CompilerParams(
            collective_id=0, has_side_effects=True, vmem_limit_bytes=48 << 20
        ),
    )(observed, psf_tiles)


def solution(mesh):
    return jax.shard_map(
        body,
        mesh=mesh,
        in_specs=(P("rng", "azi"), P("rng", "azi", None)),
        out_specs=(P("rng", "azi"), P("rng", "azi")),
        check_vma=False,
    )
```

time: 688 us -> 51.5 us (0.07)
  blocking collectives: 430 us -> 0 us
  local copies, waits for them, and re-layouts: 88.9 us -> 2.89 us
  waiting for transfers between devices: 57.3 us -> 0 us
  starting transfers between devices: 56.9 us -> 0 us
  Pallas kernels: 0 us -> 47.8 us
  matrix products: 27.1 us -> 0 us
  other arithmetic: 16.6 us -> 0 us
    psum x4 -> x0, blocking collectives: 430 us -> none  [the longest x2 221 us: grad_norm(): return lax.psum(jnp.sum(gradient * gradient), ('rng', 'azi'))]
    scatter-add x52 -> x0, local copies, waits for them, and re-layouts: 85 us -> none  [the longest x44 81.3 us: adjoint_local(): extended = extended.at[offset:offset + row_count, column_tile * TILE:colu...]
    ppermute x16 -> x0, waiting for transfers between devices: 57.3 us -> none  [the longest x4 36.2 us: padded(): lax.ppermute(lax.slice_in_dim(block, 0, width, axis=dim), axis, backward)]
    ppermute x16 -> x0, starting transfers between devices: 56.9 us -> none  [the longest x8 35.8 us: passed_along(): return lax.ppermute(block, axis, route)]
    pallas_call x0 -> x1, Pallas kernels: none -> 47.8 us  [body(): pl.pallas_call(kernel, out_shape=(block, block), in_specs=[vmem, vmem], o...]
    dot_general x45 -> x0, matrix products: 27.1 us -> none  [the longest x22 16.7 us: blur_local(): jnp.einsum('barc,abcj->arbj', window_rows, band_mats[offset], precision=l...]
    another operation x12 -> x0, other arithmetic: 9.12 us -> none
  transfers between devices with their start and end apart: 16 -> 0, of which waited for: 10 -> 0; matrix products, arithmetic and copies ran while one was open for 1% -> 0% of each run, Pallas kernels for 0% -> 0%
where the time goes in v1:
time: 51.5 us; the launch traced here: 51.3 us
  Pallas kernels  47.8 us (93%)
  local copies, waits for them, and re-layouts  2.89 us (6%)
  between operations  0.65 us (1%)
    pallas_call x1, Pallas kernels, body(): pl.pallas_call(kernel, out_shape=(block, block), in_specs=[vmem, vmem], o...  47.8 us
    unnamed x6, local copies, waits for them, and re-layouts  2.89 us

profile of v1, /device:TPU:1, one launch (start us, length us, event | category | flops | bytes accessed | tf_op | source)
XLA Modules:
  0.0 51.3 jit_solution(9513164981794029527)
XLA Ops:
  0.6 0.0 copy-start
  0.6 0.9 %copy-done = f32[128,256]{1,0:T(8,128)S(1)} copy-done((f32[128,256]{1,0:T(8,128)S(1)}, f32[128,256]{1,0:T(8,128)}, u32[]{:S(2)}) %copy-start) | copy-done | bytes 131096
  1.5 0.0 copy-start.1
  1.5 0.7 %copy-done.1 = f32[1,2,121]{2,1,0:T(2,128)S(1)} copy-done((f32[1,2,121]{2,1,0:T(2,128)S(1)}, f32[1,2,121]{2,1,0:T(2,128)}, u32[]{:S(2)}) %copy-start.1) | copy-done | bytes 992
  2.2 47.8 %shard_map.41 = (f32[128,256]{1,0:T(8,128)S(1)}, f32[128,256]{1,0:T(8,128)S(1)}) custom-call(f32[128,256]{1,0:T(8,128)S(1)} %copy-done, f32[1,2,121]{2,1,0:T(2,128)S(1)} %copy-done.1), custom_call_target="tpu_custom_call" | custom-call | tf_op jit(solution)/shard_map/pallas_call | solution.py:334
  50.0 0.7 %copy.6 = f32[128,256]{1,0:T(8,128)} copy(f32[128,256]{1,0:T(8,128)S(1)} %get-tuple-element.4) | data formatting | bytes 262144
  50.7 0.7 %copy.7 = f32[128,256]{1,0:T(8,128)} copy(f32[128,256]{1,0:T(8,128)S(1)} %get-tuple-element.5) | data formatting | bytes 262144
Async XLA Ops:
  0.6 0.9 %copy-start = (f32[128,256]{1,0:T(8,128)S(1)}, f32[128,256]{1,0:T(8,128)}, u32[]{:S(2)}) copy-start(f32[128,256]{1,0:T(8,128)} %obs_ref.1) | copy-start | bytes 393220
  1.5 0.7 %copy-start.1 = (f32[1,2,121]{2,1,0:T(2,128)S(1)}, f32[1,2,121]{2,1,0:T(2,128)}, u32[]{:S(2)}) copy-start(f32[1,2,121]{2,1,0:T(2,128)} %psf_ref.1) | copy-start | bytes 2908

commit v2 on v1

--- a/solution.py
+++ b/solution.py
@@ -21,8 +21,8 @@
 F32 = jnp.float32
 BF16 = jnp.bfloat16
 
-PARTS = {"y": 4, "zh": 4, "x": 4, "zl": 4, "c": 2}
-PHASES = (("x", "y", "c"), ("zh", "zl"))
+PARTS = {"x": 4, "y": 4, "z": 16, "c": 2}
+PHASES = (("x", "y", "c"), ("z",))
 NEIGHBOURS = tuple(
     (dr, da) for dr in (-1, 0, 1) for da in (-1, 0, 1) if (dr, da) != (0, 0)
 )
@@ -30,7 +30,11 @@
 
 def group_offsets(axes):
     ranges = [range(PARTS[axis]) for axis in axes]
-    return [dict(zip(axes, o)) for o in itertools.product(*ranges) if any(o)]
+    offsets = [dict(zip(axes, o)) for o in itertools.product(*ranges) if any(o)]
+    return sorted(
+        offsets,
+        key=lambda o: -sum(min(n, PARTS[a] - n) for a, n in o.items() if a != "c"),
+    )
 
 
 OFFSETS = tuple(group_offsets(axes) for axes in PHASES)
@@ -43,10 +47,13 @@
 
 
 def kernel(
+    obs_hbm,
+    psf_hbm,
+    grad_hbm,
+    image_hbm,
+    factors,
     obs_ref,
     psf_ref,
-    est_ref,
-    res_ref,
     taps,
     spread_w,
     gather_w,
@@ -56,6 +63,7 @@
     field,
     image,
     grad,
+    shifted,
     sides,
     got_rows,
     got_sides,
@@ -67,14 +75,18 @@
     halo_recv,
     sum_send,
     sum_recv,
+    load,
 ):
+    load_psf = pltpu.make_async_copy(psf_hbm, psf_ref, load.at[0])
+    load_obs = pltpu.make_async_copy(obs_hbm, obs_ref, load.at[1])
+    load_psf.start()
+    load_obs.start()
     rng = lax.axis_index("rng")
     azi = lax.axis_index("azi")
     place = {
+        "x": azi // 8,
         "y": rng // 4,
-        "zh": rng % 4,
-        "x": azi // 8,
-        "zl": (azi // 2) % 4,
+        "z": (rng % 4) * 4 + (azi // 2) % 4,
         "c": azi % 2,
     }
 
@@ -85,7 +97,7 @@
             else place[axis]
             for axis in PARTS
         }
-        return (at["y"] * 4 + at["zh"], at["x"] * 8 + at["zl"] * 2 + at["c"])
+        return (at["y"] * 4 + at["z"] // 4, at["x"] * 8 + (at["z"] % 4) * 2 + at["c"])
 
     def neighbour(dr, da):
         return (lax.rem(rng + dr + 16, 16), lax.rem(azi + da + 32, 32))
@@ -100,6 +112,7 @@
     row = lax.broadcasted_iota(jnp.int32, (TILE, TILE), 0)
 
     taps[...] = jnp.zeros_like(taps)
+    load_psf.wait()
     taps[0:2, 0 : KSIZE * KSIZE] = psf_ref[0]
     for t in range(2):
         gather_w[t, 3 * TILE :, :] = jnp.zeros((TILE, WIDE), BF16)
@@ -268,18 +281,19 @@
         )
         ext[...] = jnp.where(inside, ext[...], 0.0)
 
-    def square_sum(x):
-        return jnp.sum(jnp.sum(x * x, axis=0, keepdims=True), axis=1, keepdims=True)
-
-    def own_squares(turn):
-        r = lax.broadcasted_iota(jnp.int32, (EXT_ROWS, EXT_COLS), 0)
-        c = lax.broadcasted_iota(jnp.int32, (EXT_ROWS, EXT_COLS), 1)
-        own = (r >= RADIUS) & (r < ROWS + RADIUS) & (c >= RADIUS) & (c < COLS + RADIUS)
-        return square_sum(jnp.where(own, field[turn], 0.0))
+    def inner(x, y):
+        z = x * y
+        z = z[:, 0:TILE] + z[:, TILE:]
+        while z.shape[0] > 8:
+            half = z.shape[0] // 2
+            z = z[0:half] + z[half:]
+        return jnp.sum(jnp.sum(z, axis=0, keepdims=True), axis=1, keepdims=True)
 
     def own_block(turn):
-        grad[turn] = pltpu.roll(field[turn], EXT_COLS - RADIUS, 1)[:, 0:COLS]
-
+        shifted[...] = pltpu.roll(field[turn], EXT_COLS - RADIUS, 1)[:, 0:COLS]
+        grad[turn] = shifted[pl.ds(RADIUS, ROWS), :]
+
+    load_obs.wait()
     spread(obs_ref[...], spill.at[0])
     pl.semaphore_wait(barrier, len(partners))
     first = start_exchange(0)
@@ -288,18 +302,20 @@
         image[0, :, t * TILE : (t + 1) * TILE] = gather(field.at[0], t)
     spread(image[0], spill.at[1])
     second = start_exchange(1)
-    gamma = own_squares(0)
-    delta = square_sum(image[0])
     own_block(0)
+    sums = [inner(grad[0], grad[0]), inner(image[0], image[0])]
     finish_exchange(1, second)
     for t in range(2):
         image[1, :, t * TILE : (t + 1) * TILE] = gather(field.at[1], t)
-    omega = own_squares(1)
-    pi = square_sum(image[1])
+    own_block(1)
+    store_grad = pltpu.make_async_copy(grad, grad_hbm, load.at[0])
+    store_grad.start()
+    sums += [inner(grad[1], grad[1]), inner(grad[0], grad[1])]
+    sums += [inner(image[1], image[1]), inner(image[0], image[1])]
+    store_image = pltpu.make_async_copy(image, image_hbm, load.at[1])
+    store_image.start()
     line = lane[0:1]
-    moments[0] = jnp.where(
-        line == 0, gamma, jnp.where(line == 1, delta, jnp.where(line == 2, omega, pi))
-    )
+    moments[0] = sum(jnp.where(line == i, x, 0.0) for i, x in enumerate(sums))
     for phase, got in enumerate((got_a, got_b)):
         for i, o in enumerate(OFFSETS[phase]):
             pltpu.make_async_remote_copy(
@@ -310,33 +326,55 @@
                 device_id=member(o),
                 device_id_type=MESH,
             ).start()
-        if phase == 0:
-            own_block(1)
         pltpu.make_async_copy(got, got, sum_recv.at[phase]).wait()
         moments[phase + 1] = moments[phase] + jnp.sum(got[...], axis=0)
     total = moments[2]
-    gamma, delta, omega, pi = (total[:, i : i + 1] for i in range(4))
-    alpha = gamma / delta
-    rise = alpha * (omega / delta)
-    alpha_1 = (omega - delta * (delta / gamma)) / (pi - omega * (omega / delta))
+    gg, qq, ww, gw, pp, qp = (total[:, i : i + 1] for i in range(6))
+    alpha = gg / qq
+    gamma_1 = (gg - alpha * gw) - alpha * (gw - alpha * ww)
+    rise = 1.0 + gamma_1 / gg
+    delta_1 = rise * (rise * qq - alpha * qp) - alpha * (rise * qp - alpha * pp)
+    alpha_1 = gamma_1 / delta_1
     near = alpha + alpha_1 * rise
     far = alpha * alpha_1
-    own = pl.ds(RADIUS, ROWS)
-    est_ref[...] = near * grad[0, own, :] - far * grad[1, own, :]
-    res_ref[...] = obs_ref[...] - near * image[0] + far * image[1]
+    factors[...] = jnp.where(line == 0, near, far)
     for phase, got in enumerate((got_a, got_b)):
         pltpu.make_async_copy(got, got, sum_send.at[phase]).wait()
+    store_grad.wait()
+    store_image.wait()
+
+
+def finish(grad_hbm, image_hbm, obs_hbm, factors_hbm, est_hbm, res_hbm, grad, image, obs, factors, sems):
+    ins = ((factors_hbm, factors), (grad_hbm, grad), (image_hbm, image), (obs_hbm, obs))
+    loads = [pltpu.make_async_copy(a, b, sems.at[i]) for i, (a, b) in enumerate(ins)]
+    for load in loads:
+        load.start()
+    loads[0].wait()
+    loads[1].wait()
+    near, far = factors[:, 0:1], factors[:, 1:2]
+    grad[0] = near * grad[0] - far * grad[1]
+    store_est = pltpu.make_async_copy(grad.at[0], est_hbm, sems.at[4])
+    store_est.start()
+    loads[2].wait()
+    loads[3].wait()
+    image[0] = obs[...] - near * image[0] + far * image[1]
+    store_res = pltpu.make_async_copy(image.at[0], res_hbm, sems.at[5])
+    store_res.start()
+    store_est.wait()
+    store_res.wait()
 
 
 def body(observed, psf_tiles):
-    block = jax.ShapeDtypeStruct((ROWS, COLS), F32)
-    vmem = pl.BlockSpec(memory_space=pltpu.VMEM)
-    return pl.pallas_call(
+    pair = jax.ShapeDtypeStruct((2, ROWS, COLS), F32)
+    hbm = pl.BlockSpec(memory_space=pltpu.HBM)
+    grads, images, factors = pl.pallas_call(
         kernel,
-        out_shape=(block, block),
-        in_specs=[vmem, vmem],
-        out_specs=(vmem, vmem),
+        out_shape=(pair, pair, jax.ShapeDtypeStruct((1, TILE), F32)),
+        in_specs=[hbm, hbm],
+        out_specs=(hbm, hbm, pl.BlockSpec(memory_space=pltpu.VMEM)),
         scratch_shapes=[
+            pltpu.VMEM((ROWS, COLS), F32),
+            pltpu.VMEM((1, 2, KSIZE * KSIZE), F32),
             pltpu.VMEM((8, TILE), F32),
             pltpu.VMEM((2, 3 * TILE, WIDE + TILE), BF16),
             pltpu.VMEM((2, 4 * TILE, WIDE), BF16),
@@ -345,7 +383,8 @@
             pltpu.VMEM((2, EXT_ROWS, EXT_COLS), F32),
             pltpu.VMEM((2, EXT_ROWS, EXT_COLS), F32),
             pltpu.VMEM((2, ROWS, COLS), F32),
-            pltpu.VMEM((2, EXT_ROWS, COLS), F32),
+            pltpu.VMEM((2, ROWS, COLS), F32),
+            pltpu.VMEM((EXT_ROWS, COLS), F32),
             pltpu.VMEM((2, 2, 24, TILE), F32),
             pltpu.VMEM((2, 2, PAD, EXT_COLS), F32),
             pltpu.VMEM((2, 2, 24, TILE), F32),
@@ -357,11 +396,27 @@
             pltpu.SemaphoreType.DMA((2, 8)),
             pltpu.SemaphoreType.DMA((2,)),
             pltpu.SemaphoreType.DMA((2,)),
+            pltpu.SemaphoreType.DMA((2,)),
         ],
         compiler_params=pltpu.CompilerParams(
-            collective_id=0, has_side_effects=True, vmem_limit_bytes=48 << 20
+            collective_id=0, has_side_effects=True, vmem_limit_bytes=61 << 20
         ),
     )(observed, psf_tiles)
+    block = jax.ShapeDtypeStruct((ROWS, COLS), F32)
+    return pl.pallas_call(
+        finish,
+        out_shape=(block, block),
+        in_specs=[pl.BlockSpec(memory_space=pltpu.HBM)] * 4,
+        out_specs=(pl.BlockSpec(memory_space=pltpu.HBM),) * 2,
+        scratch_shapes=[
+            pltpu.VMEM((2, ROWS, COLS), F32),
+            pltpu.VMEM((2, ROWS, COLS), F32),
+            pltpu.VMEM((ROWS, COLS), F32),
+            pltpu.VMEM((1, TILE), F32),
+            pltpu.SemaphoreType.DMA((6,)),
+        ],
+        compiler_params=pltpu.CompilerParams(vmem_limit_bytes=61 << 20),
+    )(grads, images, observed, factors)
 
 
 def solution(mesh):

time: 51.5 us -> 50.9 us (0.988)
  local copies, waits for them, and re-layouts: 2.89 us -> 0 us
  Pallas kernels: 47.8 us -> 50.1 us
    unnamed x6 -> x0, local copies, waits for them, and re-layouts: 2.89 us -> none
    pallas_call x1 -> x2, Pallas kernels: 47.8 us -> 50.1 us  [the longest x1 48.3 us: body(): pl.pallas_call(kernel, out_shape=(pair, pair, jax.ShapeDtypeStruct((1, TI...]
where the time goes in v2:
time: 50.9 us; the launch traced here: 50.7 us
  Pallas kernels  50.1 us (98%)
  between operations  0.64 us (1%)
    pallas_call x1, Pallas kernels, body(): pl.pallas_call(kernel, out_shape=(pair, pair, jax.ShapeDtypeStruct((1, TI...  48.3 us
    pallas_call x1, Pallas kernels, body(): pl.pallas_call(finish, out_shape=(block, block), in_specs=[pl.BlockSpec(m...  1.8 us

profile of v2, /device:TPU:1, one launch (start us, length us, event | category | flops | bytes accessed | tf_op | source)
XLA Modules:
  0.0 50.7 jit_solution(16811397033334833972)
XLA Ops:
  0.6 48.3 %shard_map.41 = (f32[2,128,256]{2,1,0:T(8,128)}, f32[2,128,256]{2,1,0:T(8,128)}, f32[1,128]{1,0:T(1,128)}) custom-call(f32[128,256]{1,0:T(8,128)} %obs_hbm.3, f32[1,2,121]{2,1,0:T(2,128)} %psf_hbm.1), custom_call_target="tpu_custom_call" | custom-call | tf_op jit(solution)/shard_map/pallas_call | solution.py:370
  48.9 1.8 %shard_map.42 = (f32[128,256]{1,0:T(8,128)}, f32[128,256]{1,0:T(8,128)}) custom-call(f32[2,128,256]{2,1,0:T(8,128)} %get-tuple-element.5.grad_hbm, f32[2,128,256]{2,1,0:T(8,128)} %get-tuple-element.6.image_hbm, f32[128,256]{1,0:T(8,128)} %obs_hbm.3, f32[1,128]{1,0:T(1,128)} %get-tuple-element.7.factors_hbm), custom_call_target="tpu_custom_call" | custom-call | tf_op jit(solution)/shard_map/pallas_call | solution.py:406

commit v3 on v2

--- a/solution.py
+++ b/solution.py
@@ -15,7 +15,9 @@
 COLS = 256
 EXT_ROWS = 144
 EXT_COLS = 384
+TALL_ROWS = 176
 PAD = 16
+GROUPS = KSIZE * PAD
 WIDE = KSIZE * TILE
 MESH = pl.DeviceIdType.MESH
 F32 = jnp.float32
@@ -38,6 +40,126 @@
 
 
 OFFSETS = tuple(group_offsets(axes) for axes in PHASES)
+
+
+def band_group(n):
+    return (n * 373) >> 12
+
+
+def split_rows(x):
+    high = x.astype(BF16).astype(F32)
+    return high, x - high
+
+
+def iota(shape, dim):
+    return lax.broadcasted_iota(jnp.int32, shape, dim)
+
+
+def orders(taps):
+    a, b = iota((TILE, TILE), 0), iota((TILE, TILE), 1)
+    last = KSIZE * KSIZE - 1
+
+    def turned(n):
+        return KSIZE * (n - KSIZE * band_group(n)) + band_group(n)
+
+    back = last - b
+    wanted = (back, turned(b), jnp.where(back >= 0, turned(jnp.maximum(back, 0)), -1))
+    pick = [jnp.where((a == w) & (b <= last), 1.0, 0.0).astype(BF16) for w in wanted]
+    first = taps.astype(BF16)
+    rest = taps - first.astype(F32)
+    second = rest.astype(BF16)
+    third = (rest - second.astype(F32)).astype(BF16)
+    parts = jnp.concatenate([first, second, third], axis=1)
+    out = [taps]
+    for p in pick:
+        out.append(jnp.dot(parts, jnp.concatenate([p] * 3, axis=0), preferred_element_type=F32))
+    row = iota((8, TILE), 0)
+    total = out[0]
+    for k in range(1, 4):
+        total = jnp.where((row >= 2 * k) & (row < 2 * k + 2), pltpu.roll(out[k], 2 * k, 0), total)
+    return total
+
+
+def sloped(line, shift, rows):
+    base = pltpu.roll(jnp.broadcast_to(line, (8, TILE)), shift, 1)
+    return pltpu.roll(jnp.concatenate([base] * (rows // 8), axis=0), 0, 1, stride=1, stride_axis=0)
+
+
+def side_gather_weights(left, right):
+    i, n = iota((40, TILE), 0), iota((40, TILE), 1)
+    j = n - KSIZE * band_group(n)
+    halves_ = []
+    for kernel_row, start in ((left, 0), (right, 20)):
+        band = sloped(kernel_row, TILE - RIM - start, 40)
+        c = i - start
+        keep = (c >= 0) & (c < 20) & (j < RIM) & (n < 121) & (c - j >= 0) & (c - j < KSIZE)
+        halves_.append(jnp.where(keep, band, 0.0))
+    high, low = split_rows(jnp.concatenate(halves_, axis=1))
+    return jnp.concatenate([high, high, low, jnp.zeros((8, COLS), F32)], axis=0).astype(BF16)
+
+
+def side_spread_weights(left, right):
+    i, n = iota((24, TILE), 0), iota((24, TILE), 1)
+    c = n - KSIZE * band_group(n)
+    valid = (c < RIM) & (n < 121)
+    halves_ = []
+    for kernel_row, keep in (
+        (left, valid & (i < RIM) & (c <= i)),
+        (right, valid & (i >= RIM) & (i < 2 * RIM) & (c >= i - RIM)),
+    ):
+        band = sloped(kernel_row, TILE - RIM, 24)
+        halves_.append(jnp.where(keep, band, 0.0))
+    high, low = split_rows(jnp.concatenate(halves_, axis=1))
+    return jnp.concatenate([high, high, low, jnp.zeros((TILE - 72, COLS), F32)], axis=0).astype(BF16)
+
+
+def flat_gather_weights(kernel_row, low_row, high_row):
+    lane, row = iota((PAD, TILE), 1), iota((PAD, TILE), 0)
+    blocks = []
+    for v in range(KSIZE):
+        line = jnp.broadcast_to(kernel_row, (PAD, TILE))
+        line = pltpu.roll(line, TILE - KSIZE * v, 1) if v else line
+        line = jnp.where(lane < KSIZE, line, 0.0)
+        blocks.append(pltpu.roll(line, 0, 1, stride=1, stride_axis=0))
+    band = jnp.concatenate(blocks, axis=0)
+    r = jnp.concatenate([row] * KSIZE, axis=0)
+    high, low = split_rows(jnp.where((r >= low_row) & (r < high_row), band, 0.0))
+    return (high + pltpu.roll(high, 32, 1) + pltpu.roll(low, 64, 1)).astype(BF16)
+
+
+def flat_spread_weights(kernel_row, shift):
+    lane = iota((PAD, TILE), 1)
+    blocks = []
+    for v in range(KSIZE):
+        line = jnp.broadcast_to(kernel_row, (PAD, TILE))
+        line = pltpu.roll(line, (2 * TILE - (KSIZE * KSIZE - KSIZE) + KSIZE * v) % TILE, 1)
+        line = pltpu.roll(jnp.where(lane < KSIZE, line, 0.0), shift % TILE, 1)
+        line = pltpu.roll(line, 0, 1, stride=1, stride_axis=0)
+        blocks.append(jnp.where(lane < PAD, line, 0.0))
+    high, low = split_rows(jnp.concatenate(blocks, axis=0))
+    return (high + pltpu.roll(high, PAD, 1) + pltpu.roll(low, 2 * PAD, 1)).astype(BF16)
+
+
+def side_fields(near, far):
+    lane = iota(near.shape, 1)
+    left = jnp.where(lane >= TILE - RIM, far, jnp.where(lane < RIM, near, 0.0))
+    right = jnp.where(lane < 20, far, 0.0)
+    x = pltpu.roll(left, RIM, 1) + pltpu.roll(right, 20, 1)
+    high, low = split_rows(x)
+    return (high + pltpu.roll(low, 40, 1) + pltpu.roll(high, 80, 1)).astype(BF16)
+
+
+def picked(x, places, width):
+    n = iota((TILE, width), 0)
+    j = n - KSIZE * band_group(n)
+    lane = iota((TILE, width), 1)
+    blocks = [
+        jnp.where((j < RIM) & (n < 121) & (lane == j + place), 1.0, 0.0).astype(BF16)
+        for place in places
+    ]
+    pick = jnp.concatenate(blocks, axis=0)
+    high, low = halves(x)
+    return jnp.dot(jnp.concatenate([high, low], axis=1), jnp.concatenate([pick, pick], axis=0), preferred_element_type=F32)
 
 
 def halves(x):
@@ -60,14 +182,21 @@
     wide,
     tall,
     spill,
+    tall_field,
     field,
     image,
     grad,
     shifted,
-    sides,
-    got_rows,
-    got_sides,
-    got_corners,
+    stage_side,
+    stage_down,
+    stage_up,
+    got_side,
+    got_down,
+    got_up,
+    got_corner_down,
+    got_corner_up,
+    side_out,
+    side_back,
     moments,
     got_a,
     got_b,
@@ -172,10 +301,11 @@
             over = jnp.where(tall_lane < RIM, spare, 0.0)
         out[:, 2 * TILE :] = over
 
-    def gather(source, t):
+    def gather(source, row, t):
         tall_lane = lax.broadcasted_iota(jnp.int32, (EXT_ROWS, TILE), 1)
-        high, low = halves(source[:, t * TILE : (t + 1) * TILE])
-        edge = jnp.where(tall_lane < RIM, source[:, (t + 1) * TILE : (t + 2) * TILE], 0.0)
+        high, low = halves(source[row : row + EXT_ROWS, t * TILE : (t + 1) * TILE])
+        edge = source[row : row + EXT_ROWS, (t + 1) * TILE : (t + 2) * TILE]
+        edge = jnp.where(tall_lane < RIM, edge, 0.0)
         edge_high = edge.astype(BF16).astype(F32)
         edge_low = edge - edge_high
         edge = edge_high + pltpu.roll(edge_low, PAD, 1) + pltpu.roll(edge_high, 2 * PAD, 1)
@@ -191,62 +321,49 @@
             total = piece if total is None else total + piece
         return total
 
-    def pack(strip):
-        out = None
-        for k in range(8):
-            part = jnp.concatenate(
-                [
-                    strip[8 * (k + 8 * j) : 8 * (k + 8 * j) + 8]
-                    if 8 * (k + 8 * j) < EXT_ROWS
-                    else jnp.zeros((8, TILE), F32)
-                    for j in range(3)
-                ],
-                axis=0,
-            )
-            part = jnp.where(lane[0:24] < PAD, part, 0.0)
-            part = pltpu.roll(part, PAD * k, 1) if k else part
-            out = part if out is None else out + part
-        return out
-
-    def unpack(packed):
-        parts = []
-        for k in range(8):
-            part = pltpu.roll(packed, TILE - PAD * k, 1) if k else packed
-            parts.append(jnp.where(lane[0:24] < RIM, part, 0.0))
-        return jnp.concatenate(
-            [parts[g % 8][8 * (g // 8) : 8 * (g // 8) + 8] for g in range(EXT_ROWS // 8)],
-            axis=0,
+    def start_exchange():
+        side = iota((EXT_ROWS, TILE), 1)
+        kernels = orders(taps[...])
+        strips = (
+            jnp.where(side < 20, spill[:, 0:TILE], 0.0),
+            jnp.where(
+                side >= TILE - RIM,
+                spill[:, TILE : 2 * TILE],
+                jnp.where(side < RIM, spill[:, 2 * TILE :], 0.0),
+            ),
         )
-
-    def start_exchange(turn):
-        out = spill.at[turn]
-        sides[turn, 0] = pack(spill[turn, :, 0:TILE])
-        sides[turn, 1] = pack(spill[turn, :, 2 * TILE :])
-        low, high = pl.ds(0, PAD), pl.ds(ROWS, PAD)
-        first, last = pl.ds(0, TILE), pl.ds(2 * TILE, TILE)
+        for i, strip in enumerate(strips):
+            stage_side[i, 0:8] = kernels
+            stage_side[i, 8 : 8 + EXT_ROWS] = strip
+            stage_side[i, 8 + EXT_ROWS :] = kernels
+        stage_down[0:32] = spill[EXT_ROWS - 32 :]
+        stage_down[32:] = jnp.concatenate([kernels] * 3, axis=1)
+        stage_up[0:8] = jnp.concatenate([kernels] * 3, axis=1)
+        stage_up[8:] = spill[0:24]
+        whole, head, tail = pl.ds(0, 8 + EXT_ROWS), pl.ds(0, 32), pl.ds(120, 40)
         plan = {
-            (-1, 0): (out.at[low, :], got_rows.at[turn, 0]),
-            (1, 0): (out.at[high, :], got_rows.at[turn, 1]),
-            (0, -1): (sides.at[turn, 0], got_sides.at[turn, 0]),
-            (0, 1): (sides.at[turn, 1], got_sides.at[turn, 1]),
-            (-1, -1): (out.at[low, first], got_corners.at[turn, 0]),
-            (-1, 1): (out.at[low, last], got_corners.at[turn, 1]),
-            (1, -1): (out.at[high, first], got_corners.at[turn, 2]),
-            (1, 1): (out.at[high, last], got_corners.at[turn, 3]),
+            (-1, 0): (stage_up, got_up),
+            (1, 0): (stage_down, got_down),
+            (0, -1): (stage_side.at[0, whole], got_side.at[0]),
+            (0, 1): (stage_side.at[1, whole], got_side.at[1]),
+            (-1, -1): (stage_side.at[0, head], got_corner_up.at[0]),
+            (-1, 1): (stage_side.at[1, head], got_corner_up.at[1]),
+            (1, -1): (stage_side.at[0, tail], got_corner_down.at[0]),
+            (1, 1): (stage_side.at[1, tail], got_corner_down.at[1]),
         }
         copies = []
         for i, d in enumerate(NEIGHBOURS):
             source, target = plan[d]
-            copy = pltpu.make_async_remote_copy(
-                src_ref=source,
-                dst_ref=target,
-                send_sem=halo_send.at[turn, i],
-                recv_sem=halo_recv.at[turn, i],
-                device_id=neighbour(*d),
-                device_id_type=MESH,
+            copies.append(
+                pltpu.make_async_remote_copy(
+                    src_ref=source,
+                    dst_ref=target,
+                    send_sem=halo_send.at[i],
+                    recv_sem=halo_recv.at[i],
+                    device_id=neighbour(*d),
+                    device_id_type=MESH,
+                )
             )
-            copy.start()
-            copies.append(copy)
         return copies
 
     above = jnp.where(rng > 0, 1.0, 0.0)
@@ -254,32 +371,105 @@
     left_of = jnp.where(azi > 0, 1.0, 0.0)
     right_of = jnp.where(azi < 31, 1.0, 0.0)
 
-    def finish_exchange(turn, copies):
-        for copy in copies:
-            copy.wait()
-        ext = field.at[turn]
-        ext[...] = spill[turn]
-        strip_row = lax.broadcasted_iota(jnp.int32, (PAD, EXT_COLS), 0)
-        strip_lane = lax.broadcasted_iota(jnp.int32, (PAD, TILE), 1)
-        corner_row = strip_row[:, 0:TILE]
-        ext[:, 0:TILE] += unpack(got_sides[turn, 1]) * left_of
-        ext[:, 2 * TILE :] += unpack(got_sides[turn, 0]) * right_of
-        ext[0:PAD, :] += jnp.where(strip_row < RIM, got_rows[turn, 1], 0.0) * above
-        ext[ROWS:, :] += jnp.where(strip_row < RIM, got_rows[turn, 0], 0.0) * below
-        corner = (corner_row < RIM) & (strip_lane < RIM)
-        ext[0:PAD, 0:TILE] += jnp.where(corner, got_corners[turn, 3], 0.0) * (above * left_of)
-        ext[0:PAD, 2 * TILE :] += jnp.where(corner, got_corners[turn, 2], 0.0) * (above * right_of)
-        ext[ROWS:, 0:TILE] += jnp.where(corner, got_corners[turn, 1], 0.0) * (below * left_of)
-        ext[ROWS:, 2 * TILE :] += jnp.where(corner, got_corners[turn, 0], 0.0) * (below * right_of)
-        r = lax.broadcasted_iota(jnp.int32, (EXT_ROWS, EXT_COLS), 0)
-        c = lax.broadcasted_iota(jnp.int32, (EXT_ROWS, EXT_COLS), 1)
+    def assemble():
+        first, last = slice(0, TILE), slice(2 * TILE, EXT_COLS)
+        tall_field[0:PAD] = jnp.zeros((PAD, EXT_COLS), F32)
+        tall_field[PAD : PAD + EXT_ROWS] = spill[...]
+        tall_field[PAD + EXT_ROWS :] = jnp.zeros((PAD, EXT_COLS), F32)
+        tall_field[0:32] += got_down[0:32] * above
+        tall_field[144:168] += got_up[8:] * below
+
+        def from_left(strip, rows, flag):
+            lane = iota(strip.shape, 1)
+            tall_field[rows, first] += jnp.where(lane < TILE // 2, strip, 0.0) * flag
+            tall_field[rows, last] += jnp.where(lane < TILE // 2, 0.0, strip) * flag
+
+        def from_right(strip, rows, flag):
+            tall_field[rows, last] += strip * flag
+
+        middle, top, bottom = slice(16, 160), slice(0, 32), slice(144, 168)
+        from_right(got_side[0, 8:], middle, right_of)
+        from_left(got_side[1, 8:], middle, left_of)
+        from_right(got_corner_down[0, 0:32], top, above * right_of)
+        from_left(got_corner_down[1, 0:32], top, above * left_of)
+        from_right(got_corner_up[0, 8:], bottom, below * right_of)
+        from_left(got_corner_up[1, 8:], bottom, below * left_of)
+        r, c = iota((TALL_ROWS, EXT_COLS), 0), iota((TALL_ROWS, EXT_COLS), 1)
         inside = (
-            (r >= jnp.where(rng == 0, RADIUS, 0))
-            & (r < jnp.where(rng == 15, ROWS + RADIUS, EXT_ROWS))
+            (r >= jnp.where(rng == 0, PAD + RADIUS, 0))
+            & (r < jnp.where(rng == 15, PAD + RADIUS + ROWS, TALL_ROWS))
             & (c >= jnp.where(azi == 0, RADIUS, 0))
-            & (c < jnp.where(azi == 31, COLS + RADIUS, EXT_COLS))
+            & (c < jnp.where(azi == 0, 320, EXT_COLS))
+            & ((c < jnp.where(azi == 31, RADIUS + COLS, EXT_COLS)) | (c >= 320))
         )
-        ext[...] = jnp.where(inside, ext[...], 0.0)
+        tall_field[...] = jnp.where(inside, tall_field[...], 0.0)
+
+    def side_kernels(k):
+        return (
+            (got_corner_down[1, 33 + k : 34 + k] * (above * left_of), got_corner_down[0, 32 + k : 33 + k] * (above * right_of)),
+            (got_side[1, 1 + k : 2 + k] * left_of, got_side[0, k : k + 1] * right_of),
+            (got_corner_up[1, 1 + k : 2 + k] * (below * left_of), got_corner_up[0, k : k + 1] * (below * right_of)),
+        )
+
+    def side_frames():
+        fields = side_fields(tall_field[:, 0:TILE], tall_field[:, 2 * TILE :])
+        parts = ((0, 32, 144, 16), (16, 144, 0, 128), (144, 32, 176, 16))
+        group = band_group(iota((1, COLS), 1) & (TILE - 1))
+        sums = []
+        for (start, count, at, rows), (left, right) in zip(parts, side_kernels(2)):
+            side_out[at : at + count] = jnp.dot(
+                fields[start : start + count], side_gather_weights(left, right), preferred_element_type=F32
+            )
+            total = jnp.zeros((rows, COLS), F32)
+            for u in range(KSIZE):
+                total = jnp.where(group == KSIZE - 1 - u, side_out[at + u : at + u + rows], total)
+            sums.append(total)
+        frames = picked(jnp.concatenate(sums, axis=0), (0, RIM), TILE)
+        r = iota(frames.shape, 0)
+        return jnp.where((r >= 6) & (r < 154), frames, 0.0)
+
+    def side_spread(frames):
+        high, low = split_rows(frames)
+        packed = (high + pltpu.roll(low, 24, 1) + pltpu.roll(high, 48, 1)).astype(BF16)
+        for (start, stop), (left, right) in zip(((0, 16), (16, 144), (144, 160)), side_kernels(0)):
+            side_back[start:stop] = jnp.dot(
+                packed[start:stop], side_spread_weights(left, right), preferred_element_type=F32
+            )
+        group = band_group(iota((1, COLS), 1) & (TILE - 1))
+        total = jnp.zeros((EXT_ROWS, COLS), F32)
+        for u in range(KSIZE):
+            total = jnp.where(group == u, side_back[PAD - u : PAD - u + EXT_ROWS], total)
+        out = picked(total, (0, TILE), COLS)
+        return out[:, 0:TILE], out[:, TILE:]
+
+    def flat_frames(rows, kernels, low_row):
+        high, low = halves(tall_field[rows, :])
+        right = jnp.concatenate([high, low, high, jnp.zeros((32, EXT_COLS), BF16)], axis=0)
+        tiles = []
+        for t in range(2):
+            out = jnp.dot(
+                flat_gather_weights(kernels[t], low_row, low_row + RIM),
+                right[:, t * TILE : t * TILE + COLS],
+                preferred_element_type=F32,
+            )
+            total = out[0:PAD]
+            for v in range(1, KSIZE):
+                total = total + pltpu.roll(out[PAD * v : PAD * v + PAD], COLS - v, 1)
+            tiles.append(total[:, 0:TILE])
+        return tiles
+
+    def flat_spread(tiles, kernels, shift):
+        outs = []
+        for t in range(2):
+            high, low = halves(tiles[t])
+            right = jnp.concatenate([high, low, high, jnp.zeros((80, TILE), BF16)], axis=0)
+            out = jnp.dot(flat_spread_weights(kernels[t], shift), right, preferred_element_type=F32)
+            out = jnp.concatenate([out, jnp.zeros((GROUPS, TILE), F32)], axis=1)
+            total = out[0:PAD]
+            for v in range(1, KSIZE):
+                total = total + pltpu.roll(out[PAD * v : PAD * v + PAD], v, 1)
+            outs.append(total)
+        return outs
 
     def inner(x, y):
         z = x * y
@@ -289,25 +479,49 @@
             z = z[0:half] + z[half:]
         return jnp.sum(jnp.sum(z, axis=0, keepdims=True), axis=1, keepdims=True)
 
-    def own_block(turn):
-        shifted[...] = pltpu.roll(field[turn], EXT_COLS - RADIUS, 1)[:, 0:COLS]
-        grad[turn] = shifted[pl.ds(RADIUS, ROWS), :]
+    def own_block(source, row):
+        shifted[...] = pltpu.roll(source[row : row + EXT_ROWS, :], EXT_COLS - RADIUS, 1)[:, 0:COLS]
+        return shifted[pl.ds(RADIUS, ROWS), :]
 
     load_obs.wait()
-    spread(obs_ref[...], spill.at[0])
+    spread(obs_ref[...], spill)
+    copies = start_exchange()
     pl.semaphore_wait(barrier, len(partners))
-    first = start_exchange(0)
-    finish_exchange(0, first)
+    for copy in copies:
+        copy.start()
+    for copy in copies:
+        copy.wait()
+    assemble()
     for t in range(2):
-        image[0, :, t * TILE : (t + 1) * TILE] = gather(field.at[0], t)
-    spread(image[0], spill.at[1])
-    second = start_exchange(1)
-    own_block(0)
+        image[0, :, t * TILE : (t + 1) * TILE] = gather(tall_field, PAD, t)
+    frames = side_frames()
+    kernels_top = [got_down[36 + t : 37 + t, 0:TILE] * above for t in range(2)]
+    kernels_bottom = [got_up[4 + t : 5 + t, 0:TILE] * below for t in range(2)]
+    frames_top = flat_frames(slice(0, 32), kernels_top, 6)
+    frames_bottom = flat_frames(slice(144, 176), kernels_bottom, 0)
+    spread(image[0], field)
+    grad[0] = own_block(tall_field, PAD)
     sums = [inner(grad[0], grad[0]), inner(image[0], image[0])]
-    finish_exchange(1, second)
+    to_left, to_right = side_spread(frames)
+    field[:, 0:TILE] += to_left
+    field[:, 2 * TILE :] += to_right
+    kernels_top = [got_down[38 + t : 39 + t, 0:TILE] * above for t in range(2)]
+    kernels_bottom = [got_up[6 + t : 7 + t, 0:TILE] * below for t in range(2)]
+    for t, out in enumerate(flat_spread(frames_top, kernels_top, 6)):
+        field[0:PAD, t * TILE : t * TILE + COLS] += out
+    for t, out in enumerate(flat_spread(frames_bottom, kernels_bottom, -RIM)):
+        field[ROWS:, t * TILE : t * TILE + COLS] += out
+    r, c = iota((EXT_ROWS, EXT_COLS), 0), iota((EXT_ROWS, EXT_COLS), 1)
+    inside = (
+        (r >= jnp.where(rng == 0, RADIUS, 0))
+        & (r < jnp.where(rng == 15, ROWS + RADIUS, EXT_ROWS))
+        & (c >= jnp.where(azi == 0, RADIUS, 0))
+        & (c < jnp.where(azi == 31, COLS + RADIUS, EXT_COLS))
+    )
+    field[...] = jnp.where(inside, field[...], 0.0)
     for t in range(2):
-        image[1, :, t * TILE : (t + 1) * TILE] = gather(field.at[1], t)
-    own_block(1)
+        image[1, :, t * TILE : (t + 1) * TILE] = gather(field, 0, t)
+    grad[1] = own_block(field, 0)
     store_grad = pltpu.make_async_copy(grad, grad_hbm, load.at[0])
     store_grad.start()
     sums += [inner(grad[1], grad[1]), inner(grad[0], grad[1])]
@@ -380,20 +594,27 @@
             pltpu.VMEM((2, 4 * TILE, WIDE), BF16),
             pltpu.VMEM((2, ROWS + 2 * PAD, WIDE + TILE), F32),
             pltpu.VMEM((2, EXT_ROWS, WIDE), F32),
-            pltpu.VMEM((2, EXT_ROWS, EXT_COLS), F32),
-            pltpu.VMEM((2, EXT_ROWS, EXT_COLS), F32),
+            pltpu.VMEM((EXT_ROWS, EXT_COLS), F32),
+            pltpu.VMEM((TALL_ROWS, EXT_COLS), F32),
+            pltpu.VMEM((EXT_ROWS, EXT_COLS), F32),
             pltpu.VMEM((2, ROWS, COLS), F32),
             pltpu.VMEM((2, ROWS, COLS), F32),
             pltpu.VMEM((EXT_ROWS, COLS), F32),
-            pltpu.VMEM((2, 2, 24, TILE), F32),
-            pltpu.VMEM((2, 2, PAD, EXT_COLS), F32),
-            pltpu.VMEM((2, 2, 24, TILE), F32),
-            pltpu.VMEM((2, 4, PAD, TILE), F32),
+            pltpu.VMEM((2, EXT_ROWS + 16, TILE), F32),
+            pltpu.VMEM((40, EXT_COLS), F32),
+            pltpu.VMEM((32, EXT_COLS), F32),
+            pltpu.VMEM((2, EXT_ROWS + 8, TILE), F32),
+            pltpu.VMEM((40, EXT_COLS), F32),
+            pltpu.VMEM((32, EXT_COLS), F32),
+            pltpu.VMEM((2, 40, TILE), F32),
+            pltpu.VMEM((2, 32, TILE), F32),
+            pltpu.VMEM((208, COLS), F32),
+            pltpu.VMEM((160, COLS), F32),
             pltpu.VMEM((3, 1, TILE), F32),
             pltpu.VMEM((len(OFFSETS[0]), 1, TILE), F32),
             pltpu.VMEM((len(OFFSETS[1]), 1, TILE), F32),
-            pltpu.SemaphoreType.DMA((2, 8)),
-            pltpu.SemaphoreType.DMA((2, 8)),
+            pltpu.SemaphoreType.DMA((8,)),
+            pltpu.SemaphoreType.DMA((8,)),
             pltpu.SemaphoreType.DMA((2,)),
             pltpu.SemaphoreType.DMA((2,)),
             pltpu.SemaphoreType.DMA((2,)),

time: 50.9 us -> 48.6 us (0.955)
  Pallas kernels: 50.1 us -> 47.8 us
    pallas_call x1, Pallas kernels: 48.3 us -> 46 us  [body(): pl.pallas_call(kernel, out_shape=(pair, pair, jax.ShapeDtypeStruct((1, TI...]
where the time goes in v3:
time: 48.6 us; the launch traced here: 48.4 us
  Pallas kernels  47.8 us (98%)
  between operations  0.64 us (1%)
    pallas_call x1, Pallas kernels, body(): pl.pallas_call(kernel, out_shape=(pair, pair, jax.ShapeDtypeStruct((1, TI...  46 us
    pallas_call x1, Pallas kernels, body(): pl.pallas_call(finish, out_shape=(block, block), in_specs=[pl.BlockSpec(m...  1.8 us

profile of v3, /device:TPU:1, one launch (start us, length us, event | category | flops | bytes accessed | tf_op | source)
XLA Modules:
  0.0 48.4 jit_solution(15312030731853674738)
XLA Ops:
  0.6 46.0 %shard_map.41 = (f32[2,128,256]{2,1,0:T(8,128)}, f32[2,128,256]{2,1,0:T(8,128)}, f32[1,128]{1,0:T(1,128)}) custom-call(f32[128,256]{1,0:T(8,128)} %obs_hbm.3, f32[1,2,121]{2,1,0:T(2,128)} %psf_hbm.1), custom_call_target="tpu_custom_call" | custom-call | tf_op jit(solution)/shard_map/pallas_call | solution.py:584
  46.6 1.8 %shard_map.42 = (f32[128,256]{1,0:T(8,128)}, f32[128,256]{1,0:T(8,128)}) custom-call(f32[2,128,256]{2,1,0:T(8,128)} %get-tuple-element.5.grad_hbm, f32[2,128,256]{2,1,0:T(8,128)} %get-tuple-element.6.image_hbm, f32[128,256]{1,0:T(8,128)} %obs_hbm.3, f32[1,128]{1,0:T(1,128)} %get-tuple-element.7.factors_hbm), custom_call_target="tpu_custom_call" | custom-call | tf_op jit(solution)/shard_map/pallas_call | solution.py:627

commit v4 on v3

--- a/solution.py
+++ b/solution.py
@@ -187,14 +187,17 @@
     image,
     grad,
     shifted,
-    stage_side,
-    stage_down,
-    stage_up,
+    strips,
+    send_side,
+    send_up,
+    send_down,
+    send_up_corner,
+    send_down_corner,
     got_side,
+    got_up,
     got_down,
-    got_up,
-    got_corner_down,
-    got_corner_up,
+    got_up_corner,
+    got_down_corner,
     side_out,
     side_back,
     moments,
@@ -240,42 +243,76 @@
     lane = lax.broadcasted_iota(jnp.int32, (TILE, TILE), 1)
     row = lax.broadcasted_iota(jnp.int32, (TILE, TILE), 0)
 
+    edge_lane, edge_row = lane[0:PAD], row[0:PAD]
+
+    def bands(line):
+        return [
+            jnp.concatenate(
+                [pltpu.roll(part, 8 * g, 1) if g else part for g in range(TILE // 8)], axis=0
+            )
+            for part in (
+                pltpu.roll(half, 0, 1, stride=1, stride_axis=0) for half in split_rows(line)
+            )
+        ]
+
+    def taps_at(line, shift, back=0):
+        line = pltpu.roll(jnp.broadcast_to(line, (8, TILE)), (2 * TILE - shift) % TILE, 1)
+        line = jnp.where(lane[0:8] < KSIZE, line, 0.0)
+        return pltpu.roll(line, back % TILE, 1) if back else line
+
+    def build_spread():
+        for t in range(2):
+            packed = [jnp.zeros((PAD, TILE), F32)] * 2
+            for u in range(KSIZE):
+                block = slice(u * TILE, (u + 1) * TILE)
+                for k, band in enumerate(bands(taps_at(taps[t : t + 1, :], KSIZE * u))):
+                    edge = band[TILE - PAD :]
+                    below = edge_lane < edge_row + (TILE - PAD)
+                    over = jnp.where(below, edge, 0.0)
+                    packed[k] += pltpu.roll(over, RIM * u, 1) if u else over
+                    main = jnp.concatenate(
+                        [band[0 : TILE - PAD], jnp.where(below, 0.0, edge)], axis=0
+                    ).astype(BF16)
+                    if k == 0:
+                        spread_w[t, 0:TILE, block] = main
+                        spread_w[t, TILE : 2 * TILE, block] = main
+                    else:
+                        spread_w[t, 2 * TILE :, block] = main
+            blank = jnp.zeros((TILE - PAD, TILE), F32)
+            high, low = (jnp.concatenate([blank, p], axis=0).astype(BF16) for p in packed)
+            spread_w[t, 0:TILE, WIDE:] = high
+            spread_w[t, TILE : 2 * TILE, WIDE:] = high
+            spread_w[t, 2 * TILE :, WIDE:] = low
+
+    def build_gather(reverse):
+        for t in range(2):
+            gather_w[t, 3 * TILE + 3 * PAD :, :] = jnp.zeros((TILE - 3 * PAD, WIDE), BF16)
+            for u in range(KSIZE):
+                block = slice(u * TILE, (u + 1) * TILE)
+                line = taps_at(reverse[t : t + 1, :], KSIZE * (KSIZE - 1 - u), 1 - KSIZE)
+                for k, band in enumerate(bands(line)):
+                    edge = band[0:PAD]
+                    past = edge_lane > edge_row
+                    over = jnp.where(past, edge, 0.0).astype(BF16)
+                    main = jnp.concatenate(
+                        [jnp.where(past, 0.0, edge), band[PAD:]], axis=0
+                    ).astype(BF16)
+                    if k == 0:
+                        gather_w[t, 0:TILE, block] = main
+                        gather_w[t, TILE : 2 * TILE, block] = main
+                        gather_w[t, 3 * TILE : 3 * TILE + PAD, block] = over
+                        gather_w[t, 3 * TILE + PAD : 3 * TILE + 2 * PAD, block] = over
+                    else:
+                        gather_w[t, 2 * TILE : 3 * TILE, block] = main
+                        gather_w[t, 3 * TILE + 2 * PAD : 3 * TILE + 3 * PAD, block] = over
+
+    load_psf.wait()
     taps[...] = jnp.zeros_like(taps)
-    load_psf.wait()
     taps[0:2, 0 : KSIZE * KSIZE] = psf_ref[0]
-    for t in range(2):
-        gather_w[t, 3 * TILE :, :] = jnp.zeros((TILE, WIDE), BF16)
-
-        def build(u, packed, t=t):
-            line = jnp.broadcast_to(taps[t : t + 1, :], (TILE, TILE))
-            line = pltpu.roll(line, lax.rem(2 * TILE - KSIZE * u, TILE), 1)
-            line = jnp.where(lane < KSIZE, line, 0.0)
-            band = pltpu.roll(line, 0, 1, stride=1, stride_axis=0)
-            block = pl.ds(pl.multiple_of(u * TILE, TILE), TILE)
-            high, low = halves(jnp.where(lane >= row, band, 0.0))
-            spread_w[t, 0:TILE, block] = high
-            spread_w[t, TILE : 2 * TILE, block] = high
-            spread_w[t, 2 * TILE :, block] = low
-            turned = band.T
-            high, low = halves(jnp.where(row >= lane, turned, 0.0))
-            gather_w[t, 0:TILE, block] = high
-            gather_w[t, TILE : 2 * TILE, block] = high
-            gather_w[t, 2 * TILE : 3 * TILE, block] = low
-            edge = jnp.where(row < lane, turned, 0.0)[0:PAD]
-            high, low = halves(edge)
-            gather_w[t, 3 * TILE : 3 * TILE + PAD, block] = high
-            gather_w[t, 3 * TILE + PAD : 3 * TILE + 2 * PAD, block] = high
-            gather_w[t, 3 * TILE + 2 * PAD : 3 * TILE + 3 * PAD, block] = low
-            over = jnp.where(lane < row, band, 0.0)
-            return packed + pltpu.roll(over, RIM * u, 1)
-
-        packed = lax.fori_loop(0, KSIZE, build, jnp.zeros((TILE, TILE), F32))
-        high, low = halves(packed)
-        spread_w[t, 0:TILE, WIDE:] = high
-        spread_w[t, TILE : 2 * TILE, WIDE:] = high
-        spread_w[t, 2 * TILE :, WIDE:] = low
-        wide[t, 0:PAD, :] = jnp.zeros((PAD, WIDE + TILE), F32)
-        wide[t, PAD + ROWS :, :] = jnp.zeros((PAD, WIDE + TILE), F32)
+    kernels = orders(taps[...])
+    build_spread()
+    wide[:, 0:PAD, :] = jnp.zeros((2, PAD, WIDE + TILE), F32)
+    wide[:, PAD + ROWS :, :] = jnp.zeros((2, PAD, WIDE + TILE), F32)
 
     def spread(source, out):
         tall_lane = lax.broadcasted_iota(jnp.int32, (EXT_ROWS, TILE), 1)
@@ -321,50 +358,62 @@
             total = piece if total is None else total + piece
         return total
 
+    def pack(strip, rows):
+        out = None
+        for k in range(strip.shape[0] // rows):
+            part = strip[rows * k : rows * k + rows]
+            part = jnp.where(lane[0:rows] < 2 * RIM, part, 0.0)
+            part = pltpu.roll(part, 2 * RIM * k, 1) if k else part
+            out = part if out is None else out + part
+        return out
+
+    def unpack(packed, groups):
+        parts = []
+        for k in range(groups):
+            part = pltpu.roll(packed, TILE - 2 * RIM * k, 1) if k else packed
+            parts.append(jnp.where(lane[0 : packed.shape[0]] < 2 * RIM, part, 0.0))
+        return jnp.concatenate(parts, axis=0)
+
     def start_exchange():
         side = iota((EXT_ROWS, TILE), 1)
-        kernels = orders(taps[...])
-        strips = (
-            jnp.where(side < 20, spill[:, 0:TILE], 0.0),
-            jnp.where(
-                side >= TILE - RIM,
-                spill[:, TILE : 2 * TILE],
-                jnp.where(side < RIM, spill[:, 2 * TILE :], 0.0),
-            ),
-        )
-        for i, strip in enumerate(strips):
-            stage_side[i, 0:8] = kernels
-            stage_side[i, 8 : 8 + EXT_ROWS] = strip
-            stage_side[i, 8 + EXT_ROWS :] = kernels
-        stage_down[0:32] = spill[EXT_ROWS - 32 :]
-        stage_down[32:] = jnp.concatenate([kernels] * 3, axis=1)
-        stage_up[0:8] = jnp.concatenate([kernels] * 3, axis=1)
-        stage_up[8:] = spill[0:24]
-        whole, head, tail = pl.ds(0, 8 + EXT_ROWS), pl.ds(0, 32), pl.ds(120, 40)
+        right = jnp.where(side >= TILE - RIM, spill[:, TILE : 2 * TILE], spill[:, 2 * TILE :])
+        strips[0] = spill[:, 0:TILE]
+        strips[1] = pltpu.roll(right, RIM, 1)
+        for i in range(2):
+            send_side[i, 0:24] = pack(strips[i], 24)
+            send_side[i, 24:] = kernels
+            send_up_corner[i, 0:8] = pack(strips[i, 0:24], 8)
+            send_up_corner[i, 8:] = kernels
+            send_down_corner[i, 0:8] = pack(strips[i, 118:142], 8)
+            send_down_corner[i, 8:] = kernels
+        for send, at in ((send_up, 0), (send_down, 118)):
+            for t in range(2):
+                tile = slice(t * TILE, (t + 1) * TILE)
+                send[16 * t : 16 * t + 16] = spill[at : at + 16, tile]
+                send[32 + 4 * t : 36 + 4 * t] = spill[at + 16 : at + 20, tile]
+            send[40:48] = pack(spill[at : at + 24, 2 * TILE :], 8)
+            send[48:] = kernels
         plan = {
-            (-1, 0): (stage_up, got_up),
-            (1, 0): (stage_down, got_down),
-            (0, -1): (stage_side.at[0, whole], got_side.at[0]),
-            (0, 1): (stage_side.at[1, whole], got_side.at[1]),
-            (-1, -1): (stage_side.at[0, head], got_corner_up.at[0]),
-            (-1, 1): (stage_side.at[1, head], got_corner_up.at[1]),
-            (1, -1): (stage_side.at[0, tail], got_corner_down.at[0]),
-            (1, 1): (stage_side.at[1, tail], got_corner_down.at[1]),
+            (-1, 1): (send_up_corner.at[1], got_up_corner.at[1]),
+            (1, -1): (send_down_corner.at[0], got_down_corner.at[0]),
+            (-1, -1): (send_up_corner.at[0], got_up_corner.at[0]),
+            (1, 1): (send_down_corner.at[1], got_down_corner.at[1]),
+            (-1, 0): (send_up, got_up),
+            (1, 0): (send_down, got_down),
+            (0, -1): (send_side.at[0], got_side.at[0]),
+            (0, 1): (send_side.at[1], got_side.at[1]),
         }
-        copies = []
-        for i, d in enumerate(NEIGHBOURS):
-            source, target = plan[d]
-            copies.append(
-                pltpu.make_async_remote_copy(
-                    src_ref=source,
-                    dst_ref=target,
-                    send_sem=halo_send.at[i],
-                    recv_sem=halo_recv.at[i],
-                    device_id=neighbour(*d),
-                    device_id_type=MESH,
-                )
+        return [
+            pltpu.make_async_remote_copy(
+                src_ref=source,
+                dst_ref=target,
+                send_sem=halo_send.at[i],
+                recv_sem=halo_recv.at[i],
+                device_id=neighbour(*d),
+                device_id_type=MESH,
             )
-        return copies
+            for i, (d, (source, target)) in enumerate(plan.items())
+        ]
 
     above = jnp.where(rng > 0, 1.0, 0.0)
     below = jnp.where(rng < 15, 1.0, 0.0)
@@ -376,24 +425,29 @@
         tall_field[0:PAD] = jnp.zeros((PAD, EXT_COLS), F32)
         tall_field[PAD : PAD + EXT_ROWS] = spill[...]
         tall_field[PAD + EXT_ROWS :] = jnp.zeros((PAD, EXT_COLS), F32)
-        tall_field[0:32] += got_down[0:32] * above
-        tall_field[144:168] += got_up[8:] * below
+        for got, at, flag in ((got_down, 6, above), (got_up, 144, below)):
+            for t in range(2):
+                tile = slice(t * TILE, (t + 1) * TILE)
+                tall_field[at : at + 16, tile] += got[16 * t : 16 * t + 16] * flag
+                tall_field[at + 16 : at + 20, tile] += got[32 + 4 * t : 36 + 4 * t] * flag
+            tall_field[at : at + 24, last] += unpack(got[40:48], 3) * flag
 
         def from_left(strip, rows, flag):
-            lane = iota(strip.shape, 1)
-            tall_field[rows, first] += jnp.where(lane < TILE // 2, strip, 0.0) * flag
-            tall_field[rows, last] += jnp.where(lane < TILE // 2, 0.0, strip) * flag
+            strip = pltpu.roll(strip, TILE - RIM, 1) * flag
+            near = iota(strip.shape, 1) < TILE // 2
+            tall_field[rows, first] += jnp.where(near, strip, 0.0)
+            tall_field[rows, last] += jnp.where(near, 0.0, strip)
 
         def from_right(strip, rows, flag):
             tall_field[rows, last] += strip * flag
 
-        middle, top, bottom = slice(16, 160), slice(0, 32), slice(144, 168)
-        from_right(got_side[0, 8:], middle, right_of)
-        from_left(got_side[1, 8:], middle, left_of)
-        from_right(got_corner_down[0, 0:32], top, above * right_of)
-        from_left(got_corner_down[1, 0:32], top, above * left_of)
-        from_right(got_corner_up[0, 8:], bottom, below * right_of)
-        from_left(got_corner_up[1, 8:], bottom, below * left_of)
+        middle, top, bottom = slice(16, 160), slice(6, 30), slice(144, 168)
+        from_right(unpack(got_side[0, 0:24], 6), middle, right_of)
+        from_left(unpack(got_side[1, 0:24], 6), middle, left_of)
+        from_right(unpack(got_down_corner[0, 0:8], 3), top, above * right_of)
+        from_left(unpack(got_down_corner[1, 0:8], 3), top, above * left_of)
+        from_right(unpack(got_up_corner[0, 0:8], 3), bottom, below * right_of)
+        from_left(unpack(got_up_corner[1, 0:8], 3), bottom, below * left_of)
         r, c = iota((TALL_ROWS, EXT_COLS), 0), iota((TALL_ROWS, EXT_COLS), 1)
         inside = (
             (r >= jnp.where(rng == 0, PAD + RADIUS, 0))
@@ -405,10 +459,9 @@
         tall_field[...] = jnp.where(inside, tall_field[...], 0.0)
 
     def side_kernels(k):
-        return (
-            (got_corner_down[1, 33 + k : 34 + k] * (above * left_of), got_corner_down[0, 32 + k : 33 + k] * (above * right_of)),
-            (got_side[1, 1 + k : 2 + k] * left_of, got_side[0, k : k + 1] * right_of),
-            (got_corner_up[1, 1 + k : 2 + k] * (below * left_of), got_corner_up[0, k : k + 1] * (below * right_of)),
+        return tuple(
+            (got[1, at + 1 + k : at + 2 + k] * (flag * left_of), got[0, at + k : at + 1 + k] * (flag * right_of))
+            for got, at, flag in ((got_down_corner, 8, above), (got_side, 24, 1.0), (got_up_corner, 8, below))
         )
 
     def side_frames():
@@ -489,14 +542,15 @@
     pl.semaphore_wait(barrier, len(partners))
     for copy in copies:
         copy.start()
+    build_gather(kernels[2:4])
     for copy in copies:
         copy.wait()
     assemble()
     for t in range(2):
         image[0, :, t * TILE : (t + 1) * TILE] = gather(tall_field, PAD, t)
     frames = side_frames()
-    kernels_top = [got_down[36 + t : 37 + t, 0:TILE] * above for t in range(2)]
-    kernels_bottom = [got_up[4 + t : 5 + t, 0:TILE] * below for t in range(2)]
+    kernels_top = [got_down[52 + t : 53 + t] * above for t in range(2)]
+    kernels_bottom = [got_up[52 + t : 53 + t] * below for t in range(2)]
     frames_top = flat_frames(slice(0, 32), kernels_top, 6)
     frames_bottom = flat_frames(slice(144, 176), kernels_bottom, 0)
     spread(image[0], field)
@@ -505,8 +559,8 @@
     to_left, to_right = side_spread(frames)
     field[:, 0:TILE] += to_left
     field[:, 2 * TILE :] += to_right
-    kernels_top = [got_down[38 + t : 39 + t, 0:TILE] * above for t in range(2)]
-    kernels_bottom = [got_up[6 + t : 7 + t, 0:TILE] * below for t in range(2)]
+    kernels_top = [got_down[54 + t : 55 + t] * above for t in range(2)]
+    kernels_bottom = [got_up[54 + t : 55 + t] * below for t in range(2)]
     for t, out in enumerate(flat_spread(frames_top, kernels_top, 6)):
         field[0:PAD, t * TILE : t * TILE + COLS] += out
     for t, out in enumerate(flat_spread(frames_bottom, kernels_bottom, -RIM)):
@@ -600,14 +654,17 @@
             pltpu.VMEM((2, ROWS, COLS), F32),
             pltpu.VMEM((2, ROWS, COLS), F32),
             pltpu.VMEM((EXT_ROWS, COLS), F32),
-            pltpu.VMEM((2, EXT_ROWS + 16, TILE), F32),
-            pltpu.VMEM((40, EXT_COLS), F32),
-            pltpu.VMEM((32, EXT_COLS), F32),
-            pltpu.VMEM((2, EXT_ROWS + 8, TILE), F32),
-            pltpu.VMEM((40, EXT_COLS), F32),
-            pltpu.VMEM((32, EXT_COLS), F32),
-            pltpu.VMEM((2, 40, TILE), F32),
+            pltpu.VMEM((2, EXT_ROWS, TILE), F32),
             pltpu.VMEM((2, 32, TILE), F32),
+            pltpu.VMEM((56, TILE), F32),
+            pltpu.VMEM((56, TILE), F32),
+            pltpu.VMEM((2, 16, TILE), F32),
+            pltpu.VMEM((2, 16, TILE), F32),
+            pltpu.VMEM((2, 32, TILE), F32),
+            pltpu.VMEM((56, TILE), F32),
+            pltpu.VMEM((56, TILE), F32),
+            pltpu.VMEM((2, 16, TILE), F32),
+            pltpu.VMEM((2, 16, TILE), F32),
             pltpu.VMEM((208, COLS), F32),
             pltpu.VMEM((160, COLS), F32),
             pltpu.VMEM((3, 1, TILE), F32),

time: 48.6 us -> 42.7 us (0.88)
  Pallas kernels: 47.8 us -> 41.9 us
    pallas_call x1, Pallas kernels: 46 us -> 40.1 us  [body(): pl.pallas_call(kernel, out_shape=(pair, pair, jax.ShapeDtypeStruct((1, TI...]
where the time goes in v4:
time: 42.7 us; the launch traced here: 42.6 us
  Pallas kernels  41.9 us (98%)
  between operations  0.64 us (1%)
    pallas_call x1, Pallas kernels, body(): pl.pallas_call(kernel, out_shape=(pair, pair, jax.ShapeDtypeStruct((1, TI...  40.1 us
    pallas_call x1, Pallas kernels, body(): pl.pallas_call(finish, out_shape=(block, block), in_specs=[pl.BlockSpec(m...  1.8 us

profile of v4, /device:TPU:1, one launch (start us, length us, event | category | flops | bytes accessed | tf_op | source)
XLA Modules:
  0.0 42.6 jit_solution(14107276081198433824)
XLA Ops:
  0.6 40.1 %shard_map.41 = (f32[2,128,256]{2,1,0:T(8,128)}, f32[2,128,256]{2,1,0:T(8,128)}, f32[1,128]{1,0:T(1,128)}) custom-call(f32[128,256]{1,0:T(8,128)} %obs_hbm.3, f32[1,2,121]{2,1,0:T(2,128)} %psf_hbm.1), custom_call_target="tpu_custom_call" | custom-call | tf_op jit(solution)/shard_map/pallas_call | solution.py:638
  40.8 1.8 %shard_map.42 = (f32[128,256]{1,0:T(8,128)}, f32[128,256]{1,0:T(8,128)}) custom-call(f32[2,128,256]{2,1,0:T(8,128)} %get-tuple-element.5.grad_hbm, f32[2,128,256]{2,1,0:T(8,128)} %get-tuple-element.6.image_hbm, f32[128,256]{1,0:T(8,128)} %obs_hbm.3, f32[1,128]{1,0:T(1,128)} %get-tuple-element.7.factors_hbm), custom_call_target="tpu_custom_call" | custom-call | tf_op jit(solution)/shard_map/pallas_call | solution.py:684

commit v5 on v4

--- a/solution.py
+++ b/solution.py
@@ -245,71 +245,66 @@
 
     edge_lane, edge_row = lane[0:PAD], row[0:PAD]
 
-    def bands(line):
-        return [
-            jnp.concatenate(
-                [pltpu.roll(part, 8 * g, 1) if g else part for g in range(TILE // 8)], axis=0
-            )
-            for part in (
-                pltpu.roll(half, 0, 1, stride=1, stride_axis=0) for half in split_rows(line)
-            )
-        ]
-
-    def taps_at(line, shift, back=0):
-        line = pltpu.roll(jnp.broadcast_to(line, (8, TILE)), (2 * TILE - shift) % TILE, 1)
+    def band(line, shift, back):
+        line = pltpu.roll(jnp.broadcast_to(line, (8, TILE)), lax.rem(2 * TILE - shift, TILE), 1)
         line = jnp.where(lane[0:8] < KSIZE, line, 0.0)
-        return pltpu.roll(line, back % TILE, 1) if back else line
+        line = pltpu.roll(line, back, 1) if back else line
+        line = pltpu.roll(line, 0, 1, stride=1, stride_axis=0)
+        rows = [pltpu.roll(line, 8 * g, 1) if g else line for g in range(TILE // 8)]
+        return jnp.concatenate(rows, axis=0)
 
     def build_spread():
+        def one(u, packed):
+            block = pl.ds(pl.multiple_of(u * TILE, TILE), TILE)
+            out = []
+            for t in range(2):
+                rows = band(taps[t : t + 1, :], KSIZE * u, 0)
+                edge = rows[TILE - PAD :]
+                below = edge_lane < edge_row + (TILE - PAD)
+                over = jnp.where(below, edge, 0.0)
+                out.append(packed[t] + pltpu.roll(over, RIM * u, 1))
+                main = jnp.concatenate([rows[0 : TILE - PAD], jnp.where(below, 0.0, edge)], axis=0)
+                high, low = halves(main)
+                spread_w[t, 0:TILE, block] = high
+                spread_w[t, TILE : 2 * TILE, block] = high
+                spread_w[t, 2 * TILE :, block] = low
+            return tuple(out)
+
+        packed = lax.fori_loop(0, KSIZE, one, (jnp.zeros((PAD, TILE), F32),) * 2)
+        blank = jnp.zeros((TILE - PAD, TILE), BF16)
         for t in range(2):
-            packed = [jnp.zeros((PAD, TILE), F32)] * 2
-            for u in range(KSIZE):
-                block = slice(u * TILE, (u + 1) * TILE)
-                for k, band in enumerate(bands(taps_at(taps[t : t + 1, :], KSIZE * u))):
-                    edge = band[TILE - PAD :]
-                    below = edge_lane < edge_row + (TILE - PAD)
-                    over = jnp.where(below, edge, 0.0)
-                    packed[k] += pltpu.roll(over, RIM * u, 1) if u else over
-                    main = jnp.concatenate(
-                        [band[0 : TILE - PAD], jnp.where(below, 0.0, edge)], axis=0
-                    ).astype(BF16)
-                    if k == 0:
-                        spread_w[t, 0:TILE, block] = main
-                        spread_w[t, TILE : 2 * TILE, block] = main
-                    else:
-                        spread_w[t, 2 * TILE :, block] = main
-            blank = jnp.zeros((TILE - PAD, TILE), F32)
-            high, low = (jnp.concatenate([blank, p], axis=0).astype(BF16) for p in packed)
+            high, low = (jnp.concatenate([blank, p], axis=0) for p in halves(packed[t]))
             spread_w[t, 0:TILE, WIDE:] = high
             spread_w[t, TILE : 2 * TILE, WIDE:] = high
             spread_w[t, 2 * TILE :, WIDE:] = low
 
-    def build_gather(reverse):
-        for t in range(2):
-            gather_w[t, 3 * TILE + 3 * PAD :, :] = jnp.zeros((TILE - 3 * PAD, WIDE), BF16)
-            for u in range(KSIZE):
-                block = slice(u * TILE, (u + 1) * TILE)
-                line = taps_at(reverse[t : t + 1, :], KSIZE * (KSIZE - 1 - u), 1 - KSIZE)
-                for k, band in enumerate(bands(line)):
-                    edge = band[0:PAD]
-                    past = edge_lane > edge_row
-                    over = jnp.where(past, edge, 0.0).astype(BF16)
-                    main = jnp.concatenate(
-                        [jnp.where(past, 0.0, edge), band[PAD:]], axis=0
-                    ).astype(BF16)
-                    if k == 0:
-                        gather_w[t, 0:TILE, block] = main
-                        gather_w[t, TILE : 2 * TILE, block] = main
-                        gather_w[t, 3 * TILE : 3 * TILE + PAD, block] = over
-                        gather_w[t, 3 * TILE + PAD : 3 * TILE + 2 * PAD, block] = over
-                    else:
-                        gather_w[t, 2 * TILE : 3 * TILE, block] = main
-                        gather_w[t, 3 * TILE + 2 * PAD : 3 * TILE + 3 * PAD, block] = over
+    def build_gather():
+        gather_w[:, 3 * TILE + 3 * PAD :, :] = jnp.zeros((2, TILE - 3 * PAD, WIDE), BF16)
+
+        def one(u, carry):
+            block = pl.ds(pl.multiple_of(u * TILE, TILE), TILE)
+            for t in range(2):
+                rows = band(taps[2 + t : 3 + t, :], KSIZE * (KSIZE - 1) - KSIZE * u, TILE - RIM)
+                edge = rows[0:PAD]
+                past = edge_lane > edge_row
+                high, low = halves(jnp.where(past, edge, 0.0))
+                gather_w[t, 3 * TILE : 3 * TILE + PAD, block] = high
+                gather_w[t, 3 * TILE + PAD : 3 * TILE + 2 * PAD, block] = high
+                gather_w[t, 3 * TILE + 2 * PAD : 3 * TILE + 3 * PAD, block] = low
+                main = jnp.concatenate([jnp.where(past, 0.0, edge), rows[PAD:]], axis=0)
+                high, low = halves(main)
+                gather_w[t, 0:TILE, block] = high
+                gather_w[t, TILE : 2 * TILE, block] = high
+                gather_w[t, 2 * TILE : 3 * TILE, block] = low
+            return carry
+
+        lax.fori_loop(0, KSIZE, one, 0)
 
     load_psf.wait()
     taps[...] = jnp.zeros_like(taps)
     taps[0:2, 0 : KSIZE * KSIZE] = psf_ref[0]
     kernels = orders(taps[...])
+    taps[...] = kernels
     build_spread()
     wide[:, 0:PAD, :] = jnp.zeros((2, PAD, WIDE + TILE), F32)
     wide[:, PAD + ROWS :, :] = jnp.zeros((2, PAD, WIDE + TILE), F32)
@@ -542,7 +537,7 @@
     pl.semaphore_wait(barrier, len(partners))
     for copy in copies:
         copy.start()
-    build_gather(kernels[2:4])
+    build_gather()
     for copy in copies:
         copy.wait()
     assemble()

time: 42.7 us -> 42.5 us (level)
  no operation moved by 1% of the time
where the time goes in v5:
time: 42.5 us; the launch traced here: 42.3 us
  Pallas kernels  41.7 us (98%)
  between operations  0.64 us (2%)
    pallas_call x1, Pallas kernels, body(): pl.pallas_call(kernel, out_shape=(pair, pair, jax.ShapeDtypeStruct((1, TI...  39.9 us
    pallas_call x1, Pallas kernels, body(): pl.pallas_call(finish, out_shape=(block, block), in_specs=[pl.BlockSpec(m...  1.8 us

profile of v5, /device:TPU:1, one launch (start us, length us, event | category | flops | bytes accessed | tf_op | source)
XLA Modules:
  0.0 42.3 jit_solution(13902346479535418764)
XLA Ops:
  0.6 39.9 %shard_map.41 = (f32[2,128,256]{2,1,0:T(8,128)}, f32[2,128,256]{2,1,0:T(8,128)}, f32[1,128]{1,0:T(1,128)}) custom-call(f32[128,256]{1,0:T(8,128)} %obs_hbm.3, f32[1,2,121]{2,1,0:T(2,128)} %psf_hbm.1), custom_call_target="tpu_custom_call" | custom-call | tf_op jit(solution)/shard_map/pallas_call | solution.py:633
  40.6 1.8 %shard_map.42 = (f32[128,256]{1,0:T(8,128)}, f32[128,256]{1,0:T(8,128)}) custom-call(f32[2,128,256]{2,1,0:T(8,128)} %get-tuple-element.5.grad_hbm, f32[2,128,256]{2,1,0:T(8,128)} %get-tuple-element.6.image_hbm, f32[128,256]{1,0:T(8,128)} %obs_hbm.3, f32[1,128]{1,0:T(1,128)} %get-tuple-element.7.factors_hbm), custom_call_target="tpu_custom_call" | custom-call | tf_op jit(solution)/shard_map/pallas_call | solution.py:679

commit v6 on v5

--- a/solution.py
+++ b/solution.py
@@ -113,31 +113,39 @@
     return jnp.concatenate([high, high, low, jnp.zeros((TILE - 72, COLS), F32)], axis=0).astype(BF16)
 
 
-def flat_gather_weights(kernel_row, low_row, high_row):
-    lane, row = iota((PAD, TILE), 1), iota((PAD, TILE), 0)
+def flat_bands(kernel_row, order, shift, lines):
+    lane = iota((PAD, TILE), 1)
+    last = KSIZE * (KSIZE - 1)
+    base = pltpu.roll(jnp.broadcast_to(kernel_row, (8, TILE)), TILE - last, 1)
+    taps = jnp.concatenate(
+        [
+            pltpu.roll(x, 0, 1, stride=KSIZE, stride_axis=0)
+            for x in (base, pltpu.roll(base, 8 * KSIZE, 1))
+        ],
+        axis=0,
+    )
+    high, low = split_rows(jnp.where(lane < KSIZE, taps, 0.0))
+    taps = high + pltpu.roll(high, 32, 1) + pltpu.roll(low, 64, 1)
+    lines[...] = pltpu.roll(taps, shift % TILE, 1) if shift else taps
     blocks = []
-    for v in range(KSIZE):
-        line = jnp.broadcast_to(kernel_row, (PAD, TILE))
-        line = pltpu.roll(line, TILE - KSIZE * v, 1) if v else line
-        line = jnp.where(lane < KSIZE, line, 0.0)
-        blocks.append(pltpu.roll(line, 0, 1, stride=1, stride_axis=0))
-    band = jnp.concatenate(blocks, axis=0)
-    r = jnp.concatenate([row] * KSIZE, axis=0)
-    high, low = split_rows(jnp.where((r >= low_row) & (r < high_row), band, 0.0))
-    return (high + pltpu.roll(high, 32, 1) + pltpu.roll(low, 64, 1)).astype(BF16)
-
-
-def flat_spread_weights(kernel_row, shift):
-    lane = iota((PAD, TILE), 1)
-    blocks = []
-    for v in range(KSIZE):
-        line = jnp.broadcast_to(kernel_row, (PAD, TILE))
-        line = pltpu.roll(line, (2 * TILE - (KSIZE * KSIZE - KSIZE) + KSIZE * v) % TILE, 1)
-        line = pltpu.roll(jnp.where(lane < KSIZE, line, 0.0), shift % TILE, 1)
+    for v in order:
+        line = jnp.broadcast_to(lines[v : v + 1, :], (8, TILE))
         line = pltpu.roll(line, 0, 1, stride=1, stride_axis=0)
-        blocks.append(jnp.where(lane < PAD, line, 0.0))
-    high, low = split_rows(jnp.concatenate(blocks, axis=0))
-    return (high + pltpu.roll(high, PAD, 1) + pltpu.roll(low, 2 * PAD, 1)).astype(BF16)
+        blocks += [line, pltpu.roll(line, 8, 1)]
+    return jnp.concatenate(blocks, axis=0)
+
+
+def flat_gather_weights(kernel_row, low_row, high_row, lines):
+    band = flat_bands(kernel_row, range(KSIZE - 1, -1, -1), 0, lines)
+    r = iota((GROUPS, TILE), 0) & (PAD - 1)
+    return jnp.where((r >= low_row) & (r < high_row), band, 0.0).astype(BF16)
+
+
+def flat_spread_weights(kernel_row, shift, lines):
+    band = flat_bands(kernel_row, range(KSIZE), shift, lines)
+    lane = iota((GROUPS, TILE), 1)
+    keep = ((lane & 31) < PAD) & (lane < 96)
+    return jnp.where(keep, band, 0.0).astype(BF16)
 
 
 def side_fields(near, far):
@@ -149,7 +157,7 @@
     return (high + pltpu.roll(low, 40, 1) + pltpu.roll(high, 80, 1)).astype(BF16)
 
 
-def picked(x, places, width):
+def picker(places, width):
     n = iota((TILE, width), 0)
     j = n - KSIZE * band_group(n)
     lane = iota((TILE, width), 1)
@@ -157,9 +165,12 @@
         jnp.where((j < RIM) & (n < 121) & (lane == j + place), 1.0, 0.0).astype(BF16)
         for place in places
     ]
-    pick = jnp.concatenate(blocks, axis=0)
+    return jnp.concatenate(blocks * 2, axis=0)
+
+
+def picked(x, matrix):
     high, low = halves(x)
-    return jnp.dot(jnp.concatenate([high, low], axis=1), jnp.concatenate([pick, pick], axis=0), preferred_element_type=F32)
+    return jnp.dot(jnp.concatenate([high, low], axis=1), matrix, preferred_element_type=F32)
 
 
 def halves(x):
@@ -200,6 +211,9 @@
     got_down_corner,
     side_out,
     side_back,
+    lines,
+    pick_apart,
+    pick_near,
     moments,
     got_a,
     got_b,
@@ -209,10 +223,6 @@
     sum_recv,
     load,
 ):
-    load_psf = pltpu.make_async_copy(psf_hbm, psf_ref, load.at[0])
-    load_obs = pltpu.make_async_copy(obs_hbm, obs_ref, load.at[1])
-    load_psf.start()
-    load_obs.start()
     rng = lax.axis_index("rng")
     azi = lax.axis_index("azi")
     place = {
@@ -239,6 +249,10 @@
     partners += [member(o) for offsets in OFFSETS for o in offsets]
     for partner in partners:
         pl.semaphore_signal(barrier, inc=1, device_id=partner, device_id_type=MESH)
+    load_psf = pltpu.make_async_copy(psf_hbm, psf_ref, load.at[0])
+    load_obs = pltpu.make_async_copy(obs_hbm, obs_ref, load.at[1])
+    load_psf.start()
+    load_obs.start()
 
     lane = lax.broadcasted_iota(jnp.int32, (TILE, TILE), 1)
     row = lax.broadcasted_iota(jnp.int32, (TILE, TILE), 0)
@@ -262,7 +276,7 @@
                 edge = rows[TILE - PAD :]
                 below = edge_lane < edge_row + (TILE - PAD)
                 over = jnp.where(below, edge, 0.0)
-                out.append(packed[t] + pltpu.roll(over, RIM * u, 1))
+                out.append(packed[t] + pltpu.roll(over, KSIZE * u, 1))
                 main = jnp.concatenate([rows[0 : TILE - PAD], jnp.where(below, 0.0, edge)], axis=0)
                 high, low = halves(main)
                 spread_w[t, 0:TILE, block] = high
@@ -300,6 +314,8 @@
 
         lax.fori_loop(0, KSIZE, one, 0)
 
+    pick_apart[...] = picker((0, TILE), COLS)
+    pick_near[...] = picker((0, RIM), TILE)
     load_psf.wait()
     taps[...] = jnp.zeros_like(taps)
     taps[0:2, 0 : KSIZE * KSIZE] = psf_ref[0]
@@ -310,8 +326,8 @@
     wide[:, PAD + ROWS :, :] = jnp.zeros((2, PAD, WIDE + TILE), F32)
 
     def spread(source, out):
-        tall_lane = lax.broadcasted_iota(jnp.int32, (EXT_ROWS, TILE), 1)
-        over = None
+        group = band_group(iota((1, TILE), 1))
+        spares = []
         for t in range(2):
             high, low = halves(source[:, t * TILE : (t + 1) * TILE])
             left = jnp.concatenate([high, low, high], axis=1)
@@ -319,19 +335,17 @@
                 wide[t, PAD : PAD + ROWS, n : n + 256] = jnp.dot(
                     left, spread_w[t, :, n : n + 256], preferred_element_type=F32
                 )
-            total = over
-            spare = None
+            total, spare = None, jnp.zeros((EXT_ROWS, TILE), F32)
             for u in range(KSIZE):
                 rows = pl.ds(PAD - u, EXT_ROWS)
                 piece = wide[t, rows, u * TILE : (u + 1) * TILE]
                 total = piece if total is None else total + piece
-                piece = wide[t, rows, WIDE:]
-                if u:
-                    piece = pltpu.roll(piece, TILE - RIM * u, 1)
-                spare = piece if spare is None else spare + piece
+                spare = jnp.where(group == u, wide[t, rows, WIDE:], spare)
             out[:, t * TILE : (t + 1) * TILE] = total
-            over = jnp.where(tall_lane < RIM, spare, 0.0)
-        out[:, 2 * TILE :] = over
+            spares.append(spare)
+        over = picked(jnp.concatenate(spares, axis=1), pick_apart[...])
+        out[:, TILE : 2 * TILE] += over[:, 0:TILE]
+        out[:, 2 * TILE :] = over[:, TILE:]
 
     def gather(source, row, t):
         tall_lane = lax.broadcasted_iota(jnp.int32, (EXT_ROWS, TILE), 1)
@@ -472,7 +486,7 @@
             for u in range(KSIZE):
                 total = jnp.where(group == KSIZE - 1 - u, side_out[at + u : at + u + rows], total)
             sums.append(total)
-        frames = picked(jnp.concatenate(sums, axis=0), (0, RIM), TILE)
+        frames = picked(jnp.concatenate(sums, axis=0), pick_near[...])
         r = iota(frames.shape, 0)
         return jnp.where((r >= 6) & (r < 154), frames, 0.0)
 
@@ -487,16 +501,16 @@
         total = jnp.zeros((EXT_ROWS, COLS), F32)
         for u in range(KSIZE):
             total = jnp.where(group == u, side_back[PAD - u : PAD - u + EXT_ROWS], total)
-        out = picked(total, (0, TILE), COLS)
+        out = picked(total, pick_apart[...])
         return out[:, 0:TILE], out[:, TILE:]
 
-    def flat_frames(rows, kernels, low_row):
+    def flat_frames(rows, kernels, low_row, at):
         high, low = halves(tall_field[rows, :])
         right = jnp.concatenate([high, low, high, jnp.zeros((32, EXT_COLS), BF16)], axis=0)
         tiles = []
         for t in range(2):
             out = jnp.dot(
-                flat_gather_weights(kernels[t], low_row, low_row + RIM),
+                flat_gather_weights(kernels[t], low_row, low_row + RIM, lines.at[at + t]),
                 right[:, t * TILE : t * TILE + COLS],
                 preferred_element_type=F32,
             )
@@ -506,12 +520,13 @@
             tiles.append(total[:, 0:TILE])
         return tiles
 
-    def flat_spread(tiles, kernels, shift):
+    def flat_spread(tiles, kernels, shift, at):
         outs = []
         for t in range(2):
             high, low = halves(tiles[t])
-            right = jnp.concatenate([high, low, high, jnp.zeros((80, TILE), BF16)], axis=0)
-            out = jnp.dot(flat_spread_weights(kernels[t], shift), right, preferred_element_type=F32)
+            gap = jnp.zeros((PAD, TILE), BF16)
+            right = jnp.concatenate([high, gap, low, gap, high, gap, gap, gap], axis=0)
+            out = jnp.dot(flat_spread_weights(kernels[t], shift, lines.at[at + t]), right, preferred_element_type=F32)
             out = jnp.concatenate([out, jnp.zeros((GROUPS, TILE), F32)], axis=1)
             total = out[0:PAD]
             for v in range(1, KSIZE):
@@ -525,6 +540,16 @@
         while z.shape[0] > 8:
             half = z.shape[0] // 2
             z = z[0:half] + z[half:]
+        return jnp.sum(jnp.sum(z, axis=0, keepdims=True), axis=1, keepdims=True)
+
+    def inner_rimmed(x, y):
+        r, c = iota((EXT_ROWS, EXT_COLS), 0), iota((EXT_ROWS, EXT_COLS), 1)
+        own = (r >= RADIUS) & (r < ROWS + RADIUS) & (c >= RADIUS) & (c < COLS + RADIUS)
+        z = jnp.where(own, x * y, 0.0)
+        z = z[:, 0:TILE] + z[:, TILE : 2 * TILE] + z[:, 2 * TILE :]
+        z = z[0:72] + z[72:]
+        z = (z[0:24] + z[24:48]) + z[48:72]
+        z = (z[0:8] + z[8:16]) + z[16:24]
         return jnp.sum(jnp.sum(z, axis=0, keepdims=True), axis=1, keepdims=True)
 
     def own_block(source, row):
@@ -546,19 +571,17 @@
     frames = side_frames()
     kernels_top = [got_down[52 + t : 53 + t] * above for t in range(2)]
     kernels_bottom = [got_up[52 + t : 53 + t] * below for t in range(2)]
-    frames_top = flat_frames(slice(0, 32), kernels_top, 6)
-    frames_bottom = flat_frames(slice(144, 176), kernels_bottom, 0)
+    frames_top = flat_frames(slice(0, 32), kernels_top, 6, 0)
+    frames_bottom = flat_frames(slice(144, 176), kernels_bottom, 0, 2)
     spread(image[0], field)
-    grad[0] = own_block(tall_field, PAD)
-    sums = [inner(grad[0], grad[0]), inner(image[0], image[0])]
     to_left, to_right = side_spread(frames)
     field[:, 0:TILE] += to_left
     field[:, 2 * TILE :] += to_right
     kernels_top = [got_down[54 + t : 55 + t] * above for t in range(2)]
     kernels_bottom = [got_up[54 + t : 55 + t] * below for t in range(2)]
-    for t, out in enumerate(flat_spread(frames_top, kernels_top, 6)):
+    for t, out in enumerate(flat_spread(frames_top, kernels_top, 6, 4)):
         field[0:PAD, t * TILE : t * TILE + COLS] += out
-    for t, out in enumerate(flat_spread(frames_bottom, kernels_bottom, -RIM)):
+    for t, out in enumerate(flat_spread(frames_bottom, kernels_bottom, -RIM, 6)):
         field[ROWS:, t * TILE : t * TILE + COLS] += out
     r, c = iota((EXT_ROWS, EXT_COLS), 0), iota((EXT_ROWS, EXT_COLS), 1)
     inside = (
@@ -570,13 +593,13 @@
     field[...] = jnp.where(inside, field[...], 0.0)
     for t in range(2):
         image[1, :, t * TILE : (t + 1) * TILE] = gather(field, 0, t)
-    grad[1] = own_block(field, 0)
-    store_grad = pltpu.make_async_copy(grad, grad_hbm, load.at[0])
-    store_grad.start()
-    sums += [inner(grad[1], grad[1]), inner(grad[0], grad[1])]
-    sums += [inner(image[1], image[1]), inner(image[0], image[1])]
     store_image = pltpu.make_async_copy(image, image_hbm, load.at[1])
     store_image.start()
+    first = tall_field[PAD : PAD + EXT_ROWS, :]
+    second = field[...]
+    sums = [inner_rimmed(first, first), inner(image[0], image[0])]
+    sums += [inner_rimmed(second, second), inner_rimmed(first, second)]
+    sums += [inner(image[1], image[1]), inner(image[0], image[1])]
     line = lane[0:1]
     moments[0] = sum(jnp.where(line == i, x, 0.0) for i, x in enumerate(sums))
     for phase, got in enumerate((got_a, got_b)):
@@ -589,6 +612,11 @@
                 device_id=member(o),
                 device_id_type=MESH,
             ).start()
+        if phase == 0:
+            grad[0] = own_block(tall_field, PAD)
+            grad[1] = own_block(field, 0)
+            store_grad = pltpu.make_async_copy(grad, grad_hbm, load.at[0])
+            store_grad.start()
         pltpu.make_async_copy(got, got, sum_recv.at[phase]).wait()
         moments[phase + 1] = moments[phase] + jnp.sum(got[...], axis=0)
     total = moments[2]
@@ -662,6 +690,9 @@
             pltpu.VMEM((2, 16, TILE), F32),
             pltpu.VMEM((208, COLS), F32),
             pltpu.VMEM((160, COLS), F32),
+            pltpu.VMEM((8, PAD, TILE), F32),
+            pltpu.VMEM((4 * TILE, COLS), BF16),
+            pltpu.VMEM((4 * TILE, TILE), BF16),
             pltpu.VMEM((3, 1, TILE), F32),
             pltpu.VMEM((len(OFFSETS[0]), 1, TILE), F32),
             pltpu.VMEM((len(OFFSETS[1]), 1, TILE), F32),

time: 42.5 us -> 42.6 us (level)
  no operation moved by 1% of the time
where the time goes in v6:
time: 42.6 us; the launch traced here: 42.4 us
  Pallas kernels  41.8 us (98%)
  between operations  0.64 us (2%)
    pallas_call x1, Pallas kernels, body(): pl.pallas_call(kernel, out_shape=(pair, pair, jax.ShapeDtypeStruct((1, TI...  40 us
    pallas_call x1, Pallas kernels, body(): pl.pallas_call(finish, out_shape=(block, block), in_specs=[pl.BlockSpec(m...  1.8 us

profile of v6, /device:TPU:1, one launch (start us, length us, event | category | flops | bytes accessed | tf_op | source)
XLA Modules:
  0.0 42.4 jit_solution(11763124960531978650)
XLA Ops:
  0.6 40.0 %shard_map.41 = (f32[2,128,256]{2,1,0:T(8,128)}, f32[2,128,256]{2,1,0:T(8,128)}, f32[1,128]{1,0:T(1,128)}) custom-call(f32[128,256]{1,0:T(8,128)} %obs_hbm.3, f32[1,2,121]{2,1,0:T(2,128)} %psf_hbm.1), custom_call_target="tpu_custom_call" | custom-call | tf_op jit(solution)/shard_map/pallas_call | solution.py:661
  40.6 1.8 %shard_map.42 = (f32[128,256]{1,0:T(8,128)}, f32[128,256]{1,0:T(8,128)}) custom-call(f32[2,128,256]{2,1,0:T(8,128)} %get-tuple-element.5.grad_hbm, f32[2,128,256]{2,1,0:T(8,128)} %get-tuple-element.6.image_hbm, f32[128,256]{1,0:T(8,128)} %obs_hbm.3, f32[1,128]{1,0:T(1,128)} %get-tuple-element.7.factors_hbm), custom_call_target="tpu_custom_call" | custom-call | tf_op jit(solution)/shard_map/pallas_call | solution.py:710

commit v7 on v6

--- a/solution.py
+++ b/solution.py
@@ -260,7 +260,7 @@
     edge_lane, edge_row = lane[0:PAD], row[0:PAD]
 
     def band(line, shift, back):
-        line = pltpu.roll(jnp.broadcast_to(line, (8, TILE)), lax.rem(2 * TILE - shift, TILE), 1)
+        line = pltpu.roll(jnp.broadcast_to(line, (8, TILE)), lax.rem(3 * TILE - shift, TILE), 1)
         line = jnp.where(lane[0:8] < KSIZE, line, 0.0)
         line = pltpu.roll(line, back, 1) if back else line
         line = pltpu.roll(line, 0, 1, stride=1, stride_axis=0)
@@ -270,13 +270,14 @@
     def build_spread():
         def one(u, packed):
             block = pl.ds(pl.multiple_of(u * TILE, TILE), TILE)
+            used = jnp.where(u < KSIZE, 1.0, 0.0)
             out = []
             for t in range(2):
                 rows = band(taps[t : t + 1, :], KSIZE * u, 0)
                 edge = rows[TILE - PAD :]
                 below = edge_lane < edge_row + (TILE - PAD)
-                over = jnp.where(below, edge, 0.0)
-                out.append(packed[t] + pltpu.roll(over, KSIZE * u, 1))
+                over = jnp.where(below, edge, 0.0) * used
+                out.append(packed[t] + pltpu.roll(over, lax.rem(KSIZE * u, TILE), 1))
                 main = jnp.concatenate([rows[0 : TILE - PAD], jnp.where(below, 0.0, edge)], axis=0)
                 high, low = halves(main)
                 spread_w[t, 0:TILE, block] = high
@@ -284,7 +285,12 @@
                 spread_w[t, 2 * TILE :, block] = low
             return tuple(out)
 
-        packed = lax.fori_loop(0, KSIZE, one, (jnp.zeros((PAD, TILE), F32),) * 2)
+        def three(i, packed):
+            for k in range(3):
+                packed = one(3 * i + k, packed)
+            return packed
+
+        packed = lax.fori_loop(0, 4, three, (jnp.zeros((PAD, TILE), F32),) * 2)
         blank = jnp.zeros((TILE - PAD, TILE), BF16)
         for t in range(2):
             high, low = (jnp.concatenate([blank, p], axis=0) for p in halves(packed[t]))
@@ -293,7 +299,7 @@
             spread_w[t, 2 * TILE :, WIDE:] = low
 
     def build_gather():
-        gather_w[:, 3 * TILE + 3 * PAD :, :] = jnp.zeros((2, TILE - 3 * PAD, WIDE), BF16)
+        gather_w[:, 3 * TILE + 3 * PAD :, :] = jnp.zeros((2, TILE - 3 * PAD, WIDE + TILE), BF16)
 
         def one(u, carry):
             block = pl.ds(pl.multiple_of(u * TILE, TILE), TILE)
@@ -312,7 +318,12 @@
                 gather_w[t, 2 * TILE : 3 * TILE, block] = low
             return carry
 
-        lax.fori_loop(0, KSIZE, one, 0)
+        def three(i, carry):
+            for k in range(3):
+                one(3 * i + k, carry)
+            return carry
+
+        lax.fori_loop(0, 4, three, 0)
 
     pick_apart[...] = picker((0, TILE), COLS)
     pick_near[...] = picker((0, RIM), TILE)
@@ -527,10 +538,14 @@
             gap = jnp.zeros((PAD, TILE), BF16)
             right = jnp.concatenate([high, gap, low, gap, high, gap, gap, gap], axis=0)
             out = jnp.dot(flat_spread_weights(kernels[t], shift, lines.at[at + t]), right, preferred_element_type=F32)
-            out = jnp.concatenate([out, jnp.zeros((GROUPS, TILE), F32)], axis=1)
-            total = out[0:PAD]
+            near, far = out[0:PAD], None
             for v in range(1, KSIZE):
-                total = total + pltpu.roll(out[PAD * v : PAD * v + PAD], v, 1)
+                piece = pltpu.roll(out[PAD * v : PAD * v + PAD], v, 1)
+                past = edge_lane < v
+                near = near + jnp.where(past, 0.0, piece)
+                piece = jnp.where(past, piece, 0.0)
+                far = piece if far is None else far + piece
+            total = jnp.concatenate([near, far], axis=1)
             outs.append(total)
         return outs
 
@@ -668,7 +683,7 @@
             pltpu.VMEM((1, 2, KSIZE * KSIZE), F32),
             pltpu.VMEM((8, TILE), F32),
             pltpu.VMEM((2, 3 * TILE, WIDE + TILE), BF16),
-            pltpu.VMEM((2, 4 * TILE, WIDE), BF16),
+            pltpu.VMEM((2, 4 * TILE, WIDE + TILE), BF16),
             pltpu.VMEM((2, ROWS + 2 * PAD, WIDE + TILE), F32),
             pltpu.VMEM((2, EXT_ROWS, WIDE), F32),
             pltpu.VMEM((EXT_ROWS, EXT_COLS), F32),

time: 42.6 us -> 42 us (0.986)
  Pallas kernels: 41.8 us -> 41.3 us
    pallas_call x1, Pallas kernels: 40 us -> 39.5 us  [body(): pl.pallas_call(kernel, out_shape=(pair, pair, jax.ShapeDtypeStruct((1, TI...]
where the time goes in v7:
time: 42 us; the launch traced here: 41.9 us
  Pallas kernels  41.3 us (98%)
  between operations  0.64 us (2%)
    pallas_call x1, Pallas kernels, body(): pl.pallas_call(kernel, out_shape=(pair, pair, jax.ShapeDtypeStruct((1, TI...  39.5 us
    pallas_call x1, Pallas kernels, body(): pl.pallas_call(finish, out_shape=(block, block), in_specs=[pl.BlockSpec(m...  1.8 us

profile of v7, /device:TPU:1, one launch (start us, length us, event | category | flops | bytes accessed | tf_op | source)
XLA Modules:
  0.0 41.9 jit_solution(9204452967403952439)
XLA Ops:
  0.6 39.5 %shard_map.41 = (f32[2,128,256]{2,1,0:T(8,128)}, f32[2,128,256]{2,1,0:T(8,128)}, f32[1,128]{1,0:T(1,128)}) custom-call(f32[128,256]{1,0:T(8,128)} %obs_hbm.3, f32[1,2,121]{2,1,0:T(2,128)} %psf_hbm.1), custom_call_target="tpu_custom_call" | custom-call | tf_op jit(solution)/shard_map/pallas_call | solution.py:676
  40.1 1.8 %shard_map.42 = (f32[128,256]{1,0:T(8,128)}, f32[128,256]{1,0:T(8,128)}) custom-call(f32[2,128,256]{2,1,0:T(8,128)} %get-tuple-element.5.grad_hbm, f32[2,128,256]{2,1,0:T(8,128)} %get-tuple-element.6.image_hbm, f32[128,256]{1,0:T(8,128)} %obs_hbm.3, f32[1,128]{1,0:T(1,128)} %get-tuple-element.7.factors_hbm), custom_call_target="tpu_custom_call" | custom-call | tf_op jit(solution)/shard_map/pallas_call | solution.py:725

commit v8 on v7

--- a/solution.py
+++ b/solution.py
@@ -212,6 +212,8 @@
     side_out,
     side_back,
     lines,
+    flat_w,
+    side_w,
     pick_apart,
     pick_near,
     moments,
@@ -285,12 +287,12 @@
                 spread_w[t, 2 * TILE :, block] = low
             return tuple(out)
 
-        def three(i, packed):
-            for k in range(3):
-                packed = one(3 * i + k, packed)
+        def six(i, packed):
+            for k in range(6):
+                packed = one(6 * i + k, packed)
             return packed
 
-        packed = lax.fori_loop(0, 4, three, (jnp.zeros((PAD, TILE), F32),) * 2)
+        packed = lax.fori_loop(0, 2, six, (jnp.zeros((PAD, TILE), F32),) * 2)
         blank = jnp.zeros((TILE - PAD, TILE), BF16)
         for t in range(2):
             high, low = (jnp.concatenate([blank, p], axis=0) for p in halves(packed[t]))
@@ -318,12 +320,12 @@
                 gather_w[t, 2 * TILE : 3 * TILE, block] = low
             return carry
 
-        def three(i, carry):
-            for k in range(3):
-                one(3 * i + k, carry)
+        def six(i, carry):
+            for k in range(6):
+                one(6 * i + k, carry)
             return carry
 
-        lax.fori_loop(0, 4, three, 0)
+        lax.fori_loop(0, 2, six, 0)
 
     pick_apart[...] = picker((0, TILE), COLS)
     pick_near[...] = picker((0, RIM), TILE)
@@ -440,7 +442,19 @@
     left_of = jnp.where(azi > 0, 1.0, 0.0)
     right_of = jnp.where(azi < 31, 1.0, 0.0)
 
-    def assemble():
+    def prepare_frames():
+        for t in range(2):
+            for at, got, flag, low_row, shift in ((0, got_down, above, 6, 6), (2, got_up, below, 0, -RIM)):
+                flat_w[at + t] = flat_gather_weights(
+                    got[52 + t : 53 + t] * flag, low_row, low_row + RIM, lines.at[at + t]
+                )
+                flat_w[4 + at + t] = flat_spread_weights(
+                    got[54 + t : 55 + t] * flag, shift, lines.at[4 + at + t]
+                )
+        side_w[0] = side_gather_weights(*side_kernels(2)[1])
+        side_w[1] = side_spread_weights(*side_kernels(0)[1])
+
+    def assemble(corners):
         first, last = slice(0, TILE), slice(2 * TILE, EXT_COLS)
         tall_field[0:PAD] = jnp.zeros((PAD, EXT_COLS), F32)
         tall_field[PAD : PAD + EXT_ROWS] = spill[...]
@@ -464,6 +478,8 @@
         middle, top, bottom = slice(16, 160), slice(6, 30), slice(144, 168)
         from_right(unpack(got_side[0, 0:24], 6), middle, right_of)
         from_left(unpack(got_side[1, 0:24], 6), middle, left_of)
+        for copy in corners:
+            copy.wait()
         from_right(unpack(got_down_corner[0, 0:8], 3), top, above * right_of)
         from_left(unpack(got_down_corner[1, 0:8], 3), top, above * left_of)
         from_right(unpack(got_up_corner[0, 0:8], 3), bottom, below * right_of)
@@ -491,7 +507,9 @@
         sums = []
         for (start, count, at, rows), (left, right) in zip(parts, side_kernels(2)):
             side_out[at : at + count] = jnp.dot(
-                fields[start : start + count], side_gather_weights(left, right), preferred_element_type=F32
+                fields[start : start + count],
+                side_w[0] if start == PAD else side_gather_weights(left, right),
+                preferred_element_type=F32,
             )
             total = jnp.zeros((rows, COLS), F32)
             for u in range(KSIZE):
@@ -506,7 +524,9 @@
         packed = (high + pltpu.roll(low, 24, 1) + pltpu.roll(high, 48, 1)).astype(BF16)
         for (start, stop), (left, right) in zip(((0, 16), (16, 144), (144, 160)), side_kernels(0)):
             side_back[start:stop] = jnp.dot(
-                packed[start:stop], side_spread_weights(left, right), preferred_element_type=F32
+                packed[start:stop],
+                side_w[1] if start == PAD else side_spread_weights(left, right),
+                preferred_element_type=F32,
             )
         group = band_group(iota((1, COLS), 1) & (TILE - 1))
         total = jnp.zeros((EXT_ROWS, COLS), F32)
@@ -515,13 +535,13 @@
         out = picked(total, pick_apart[...])
         return out[:, 0:TILE], out[:, TILE:]
 
-    def flat_frames(rows, kernels, low_row, at):
+    def flat_frames(rows, at):
         high, low = halves(tall_field[rows, :])
         right = jnp.concatenate([high, low, high, jnp.zeros((32, EXT_COLS), BF16)], axis=0)
         tiles = []
         for t in range(2):
             out = jnp.dot(
-                flat_gather_weights(kernels[t], low_row, low_row + RIM, lines.at[at + t]),
+                flat_w[at + t],
                 right[:, t * TILE : t * TILE + COLS],
                 preferred_element_type=F32,
             )
@@ -531,13 +551,13 @@
             tiles.append(total[:, 0:TILE])
         return tiles
 
-    def flat_spread(tiles, kernels, shift, at):
+    def flat_spread(tiles, at):
         outs = []
         for t in range(2):
             high, low = halves(tiles[t])
             gap = jnp.zeros((PAD, TILE), BF16)
             right = jnp.concatenate([high, gap, low, gap, high, gap, gap, gap], axis=0)
-            out = jnp.dot(flat_spread_weights(kernels[t], shift, lines.at[at + t]), right, preferred_element_type=F32)
+            out = jnp.dot(flat_w[at + t], right, preferred_element_type=F32)
             near, far = out[0:PAD], None
             for v in range(1, KSIZE):
                 piece = pltpu.roll(out[PAD * v : PAD * v + PAD], v, 1)
@@ -578,25 +598,22 @@
     for copy in copies:
         copy.start()
     build_gather()
-    for copy in copies:
+    for copy in copies[4:]:
         copy.wait()
-    assemble()
+    prepare_frames()
+    assemble(copies[:4])
     for t in range(2):
         image[0, :, t * TILE : (t + 1) * TILE] = gather(tall_field, PAD, t)
     frames = side_frames()
-    kernels_top = [got_down[52 + t : 53 + t] * above for t in range(2)]
-    kernels_bottom = [got_up[52 + t : 53 + t] * below for t in range(2)]
-    frames_top = flat_frames(slice(0, 32), kernels_top, 6, 0)
-    frames_bottom = flat_frames(slice(144, 176), kernels_bottom, 0, 2)
+    frames_top = flat_frames(slice(0, 32), 0)
+    frames_bottom = flat_frames(slice(144, 176), 2)
     spread(image[0], field)
     to_left, to_right = side_spread(frames)
     field[:, 0:TILE] += to_left
     field[:, 2 * TILE :] += to_right
-    kernels_top = [got_down[54 + t : 55 + t] * above for t in range(2)]
-    kernels_bottom = [got_up[54 + t : 55 + t] * below for t in range(2)]
-    for t, out in enumerate(flat_spread(frames_top, kernels_top, 6, 4)):
+    for t, out in enumerate(flat_spread(frames_top, 4)):
         field[0:PAD, t * TILE : t * TILE + COLS] += out
-    for t, out in enumerate(flat_spread(frames_bottom, kernels_bottom, -RIM, 6)):
+    for t, out in enumerate(flat_spread(frames_bottom, 6)):
         field[ROWS:, t * TILE : t * TILE + COLS] += out
     r, c = iota((EXT_ROWS, EXT_COLS), 0), iota((EXT_ROWS, EXT_COLS), 1)
     inside = (
@@ -706,6 +723,8 @@
             pltpu.VMEM((208, COLS), F32),
             pltpu.VMEM((160, COLS), F32),
             pltpu.VMEM((8, PAD, TILE), F32),
+            pltpu.VMEM((8, GROUPS, TILE), BF16),
+            pltpu.VMEM((2, TILE, COLS), BF16),
             pltpu.VMEM((4 * TILE, COLS), BF16),
             pltpu.VMEM((4 * TILE, TILE), BF16),
             pltpu.VMEM((3, 1, TILE), F32),

time: 42 us -> 42.2 us (level)
  no operation moved by 1% of the time
where the time goes in v8:
time: 42.2 us; the launch traced here: 42 us
  Pallas kernels  41.4 us (98%)
  between operations  0.64 us (2%)
    pallas_call x1, Pallas kernels, body(): pl.pallas_call(kernel, out_shape=(pair, pair, jax.ShapeDtypeStruct((1, TI...  39.6 us
    pallas_call x1, Pallas kernels, body(): pl.pallas_call(finish, out_shape=(block, block), in_specs=[pl.BlockSpec(m...  1.8 us

profile of v8, /device:TPU:1, one launch (start us, length us, event | category | flops | bytes accessed | tf_op | source)
XLA Modules:
  0.0 42.0 jit_solution(13624421476924441570)
XLA Ops:
  0.6 39.6 %shard_map.41 = (f32[2,128,256]{2,1,0:T(8,128)}, f32[2,128,256]{2,1,0:T(8,128)}, f32[1,128]{1,0:T(1,128)}) custom-call(f32[128,256]{1,0:T(8,128)} %obs_hbm.3, f32[1,2,121]{2,1,0:T(2,128)} %psf_hbm.1), custom_call_target="tpu_custom_call" | custom-call | tf_op jit(solution)/shard_map/pallas_call | solution.py:693
  40.2 1.8 %shard_map.42 = (f32[128,256]{1,0:T(8,128)}, f32[128,256]{1,0:T(8,128)}) custom-call(f32[2,128,256]{2,1,0:T(8,128)} %get-tuple-element.5.grad_hbm, f32[2,128,256]{2,1,0:T(8,128)} %get-tuple-element.6.image_hbm, f32[128,256]{1,0:T(8,128)} %obs_hbm.3, f32[1,128]{1,0:T(1,128)} %get-tuple-element.7.factors_hbm), custom_call_target="tpu_custom_call" | custom-call | tf_op jit(solution)/shard_map/pallas_call | solution.py:744

commit v9 on v8

--- a/solution.py
+++ b/solution.py
@@ -479,7 +479,7 @@
         from_right(unpack(got_side[0, 0:24], 6), middle, right_of)
         from_left(unpack(got_side[1, 0:24], 6), middle, left_of)
         for copy in corners:
-            copy.wait()
+            copy.wait_recv()
         from_right(unpack(got_down_corner[0, 0:8], 3), top, above * right_of)
         from_left(unpack(got_down_corner[1, 0:8], 3), top, above * left_of)
         from_right(unpack(got_up_corner[0, 0:8], 3), bottom, below * right_of)
@@ -599,7 +599,7 @@
         copy.start()
     build_gather()
     for copy in copies[4:]:
-        copy.wait()
+        copy.wait_recv()
     prepare_frames()
     assemble(copies[:4])
     for t in range(2):
@@ -663,25 +663,28 @@
     factors[...] = jnp.where(line == 0, near, far)
     for phase, got in enumerate((got_a, got_b)):
         pltpu.make_async_copy(got, got, sum_send.at[phase]).wait()
+    for copy in copies:
+        copy.wait_send()
     store_grad.wait()
     store_image.wait()
 
 
 def finish(grad_hbm, image_hbm, obs_hbm, factors_hbm, est_hbm, res_hbm, grad, image, obs, factors, sems):
-    ins = ((factors_hbm, factors), (grad_hbm, grad), (image_hbm, image), (obs_hbm, obs))
+    ins = [(factors_hbm, factors), (grad_hbm.at[0], grad.at[0]), (grad_hbm.at[1], grad.at[1])]
+    ins += [(image_hbm.at[0], image.at[0]), (image_hbm.at[1], image.at[1]), (obs_hbm, obs)]
     loads = [pltpu.make_async_copy(a, b, sems.at[i]) for i, (a, b) in enumerate(ins)]
     for load in loads:
         load.start()
-    loads[0].wait()
-    loads[1].wait()
+    for load in loads[:3]:
+        load.wait()
     near, far = factors[:, 0:1], factors[:, 1:2]
     grad[0] = near * grad[0] - far * grad[1]
-    store_est = pltpu.make_async_copy(grad.at[0], est_hbm, sems.at[4])
+    store_est = pltpu.make_async_copy(grad.at[0], est_hbm, sems.at[6])
     store_est.start()
-    loads[2].wait()
-    loads[3].wait()
+    for load in loads[3:]:
+        load.wait()
     image[0] = obs[...] - near * image[0] + far * image[1]
-    store_res = pltpu.make_async_copy(image.at[0], res_hbm, sems.at[5])
+    store_res = pltpu.make_async_copy(image.at[0], res_hbm, sems.at[7])
     store_res.start()
     store_est.wait()
     store_res.wait()
@@ -751,7 +754,7 @@
             pltpu.VMEM((2, ROWS, COLS), F32),
             pltpu.VMEM((ROWS, COLS), F32),
             pltpu.VMEM((1, TILE), F32),
-            pltpu.SemaphoreType.DMA((6,)),
+            pltpu.SemaphoreType.DMA((8,)),
         ],
         compiler_params=pltpu.CompilerParams(vmem_limit_bytes=61 << 20),
     )(grads, images, observed, factors)

time: 42.2 us -> 42.3 us (level)
  no operation moved by 1% of the time
where the time goes in v9:
time: 42.3 us; the launch traced here: 42.2 us
  Pallas kernels  41.5 us (98%)
  between operations  0.64 us (2%)
    pallas_call x1, Pallas kernels, body(): pl.pallas_call(kernel, out_shape=(pair, pair, jax.ShapeDtypeStruct((1, TI...  39.6 us
    pallas_call x1, Pallas kernels, body(): pl.pallas_call(finish, out_shape=(block, block), in_specs=[pl.BlockSpec(m...  1.91 us

profile of v9, /device:TPU:1, one launch (start us, length us, event | category | flops | bytes accessed | tf_op | source)
XLA Modules:
  0.0 42.2 jit_solution(5268935925810701470)
XLA Ops:
  0.6 39.6 %shard_map.41 = (f32[2,128,256]{2,1,0:T(8,128)}, f32[2,128,256]{2,1,0:T(8,128)}, f32[1,128]{1,0:T(1,128)}) custom-call(f32[128,256]{1,0:T(8,128)} %obs_hbm.3, f32[1,2,121]{2,1,0:T(2,128)} %psf_hbm.1), custom_call_target="tpu_custom_call" | custom-call | tf_op jit(solution)/shard_map/pallas_call | solution.py:696
  40.2 1.9 %shard_map.42 = (f32[128,256]{1,0:T(8,128)}, f32[128,256]{1,0:T(8,128)}) custom-call(f32[2,128,256]{2,1,0:T(8,128)} %get-tuple-element.5.grad_hbm, f32[2,128,256]{2,1,0:T(8,128)} %get-tuple-element.6.image_hbm, f32[128,256]{1,0:T(8,128)} %obs_hbm.3, f32[1,128]{1,0:T(1,128)} %get-tuple-element.7.factors_hbm), custom_call_target="tpu_custom_call" | custom-call | tf_op jit(solution)/shard_map/pallas_call | solution.py:747

commit v10 on v7

--- a/solution.py
+++ b/solution.py
@@ -245,14 +245,16 @@
         return (lax.rem(rng + dr + 16, 16), lax.rem(azi + da + 32, 32))
 
     barrier = pltpu.get_barrier_semaphore()
-    partners = [neighbour(*d) for d in NEIGHBOURS]
-    partners += [member(o) for offsets in OFFSETS for o in offsets]
-    for partner in partners:
+    near_by = [neighbour(*d) for d in NEIGHBOURS]
+    partners = near_by + [member(o) for offsets in OFFSETS for o in offsets]
+    for partner in near_by:
         pl.semaphore_signal(barrier, inc=1, device_id=partner, device_id_type=MESH)
     load_psf = pltpu.make_async_copy(psf_hbm, psf_ref, load.at[0])
     load_obs = pltpu.make_async_copy(obs_hbm, obs_ref, load.at[1])
     load_psf.start()
     load_obs.start()
+    for partner in partners[len(near_by) :]:
+        pl.semaphore_signal(barrier, inc=1, device_id=partner, device_id_type=MESH)
 
     lane = lax.broadcasted_iota(jnp.int32, (TILE, TILE), 1)
     row = lax.broadcasted_iota(jnp.int32, (TILE, TILE), 0)

time: 42 us -> 42.1 us (level)
  no operation moved by 1% of the time
where the time goes in v10:
time: 42.1 us; the launch traced here: 42 us
  Pallas kernels  41.4 us (98%)
  between operations  0.64 us (2%)
    pallas_call x1, Pallas kernels, body(): pl.pallas_call(kernel, out_shape=(pair, pair, jax.ShapeDtypeStruct((1, TI...  39.6 us
    pallas_call x1, Pallas kernels, body(): pl.pallas_call(finish, out_shape=(block, block), in_specs=[pl.BlockSpec(m...  1.8 us

profile of v10, /device:TPU:1, one launch (start us, length us, event | category | flops | bytes accessed | tf_op | source)
XLA Modules:
  0.0 42.0 jit_solution(5964113270797257297)
XLA Ops:
  0.6 39.6 %shard_map.41 = (f32[2,128,256]{2,1,0:T(8,128)}, f32[2,128,256]{2,1,0:T(8,128)}, f32[1,128]{1,0:T(1,128)}) custom-call(f32[128,256]{1,0:T(8,128)} %obs_hbm.3, f32[1,2,121]{2,1,0:T(2,128)} %psf_hbm.1), custom_call_target="tpu_custom_call" | custom-call | tf_op jit(solution)/shard_map/pallas_call | solution.py:678
  40.2 1.8 %shard_map.42 = (f32[128,256]{1,0:T(8,128)}, f32[128,256]{1,0:T(8,128)}) custom-call(f32[2,128,256]{2,1,0:T(8,128)} %get-tuple-element.5.grad_hbm, f32[2,128,256]{2,1,0:T(8,128)} %get-tuple-element.6.image_hbm, f32[128,256]{1,0:T(8,128)} %obs_hbm.3, f32[1,128]{1,0:T(1,128)} %get-tuple-element.7.factors_hbm), custom_call_target="tpu_custom_call" | custom-call | tf_op jit(solution)/shard_map/pallas_call | solution.py:727

commit v11 on v7

--- a/solution.py
+++ b/solution.py
@@ -24,7 +24,7 @@
 BF16 = jnp.bfloat16
 
 PARTS = {"x": 4, "y": 4, "z": 16, "c": 2}
-PHASES = (("x", "y", "c"), ("z",))
+PHASES = (("z", "c"), ("x", "y"))
 NEIGHBOURS = tuple(
     (dr, da) for dr in (-1, 0, 1) for da in (-1, 0, 1) if (dr, da) != (0, 0)
 )

time: 42 us -> 42.3 us (level)
  no operation moved by 1% of the time
where the time goes in v11:
time: 42.3 us; the launch traced here: 42.1 us
  Pallas kernels  41.5 us (98%)
  between operations  0.64 us (2%)
    pallas_call x1, Pallas kernels, body(): pl.pallas_call(kernel, out_shape=(pair, pair, jax.ShapeDtypeStruct((1, TI...  39.7 us
    pallas_call x1, Pallas kernels, body(): pl.pallas_call(finish, out_shape=(block, block), in_specs=[pl.BlockSpec(m...  1.8 us

profile of v11, /device:TPU:1, one launch (start us, length us, event | category | flops | bytes accessed | tf_op | source)
XLA Modules:
  0.0 42.1 jit_solution(3912640351951043450)
XLA Ops:
  0.6 39.7 %shard_map.41 = (f32[2,128,256]{2,1,0:T(8,128)}, f32[2,128,256]{2,1,0:T(8,128)}, f32[1,128]{1,0:T(1,128)}) custom-call(f32[128,256]{1,0:T(8,128)} %obs_hbm.3, f32[1,2,121]{2,1,0:T(2,128)} %psf_hbm.1), custom_call_target="tpu_custom_call" | custom-call | tf_op jit(solution)/shard_map/pallas_call | solution.py:676
  40.4 1.8 %shard_map.42 = (f32[128,256]{1,0:T(8,128)}, f32[128,256]{1,0:T(8,128)}) custom-call(f32[2,128,256]{2,1,0:T(8,128)} %get-tuple-element.5.grad_hbm, f32[2,128,256]{2,1,0:T(8,128)} %get-tuple-element.6.image_hbm, f32[128,256]{1,0:T(8,128)} %obs_hbm.3, f32[1,128]{1,0:T(1,128)} %get-tuple-element.7.factors_hbm), custom_call_target="tpu_custom_call" | custom-call | tf_op jit(solution)/shard_map/pallas_call | solution.py:725
